TPU v7x, 32 devices: a whole 2x2x4 slice. The times are simulated.
32 devices in a mesh: branch: 2 (over x), strip: 16 (over z, y, core).
Axes of the slice: x: 2, y: 2, z: 4, core: 2. Of those that a mesh axis runs over, the one named last changes fastest.
Arguments:
- image_feats: bfloat16 [32, 2048, 256], P(None, ('branch', 'strip')), may hold values from -6 to 6
- cam_weights: bfloat16 [3, 9, 256, 256], replicated, may hold values from -0.1875 to 0.1875
- depth_weight: bfloat16 [256, 118], replicated, may hold values from -1.5 to 1.5
- ray_bins: int32 [2048, 118], P(('branch', 'strip')), may hold values from 0 to 2047, as said below
- pillar_sums: bfloat16 [32, 256, 128], P(None, ('branch', 'strip')), may hold values from -12 to 12
- pillar_counts: int32 [32, 256], P(None, ('branch', 'strip')), may hold values from 0 to 8
- lidar_weight: bfloat16 [4, 128, 128], replicated, may hold values from -0.375 to 0.375
- merge_weight: bfloat16 [9, 384, 256], replicated, may hold values from -0.15625 to 0.15625
- out_cotangent: bfloat16 [16, 128, 256], P(None, ('branch', 'strip')), may hold values from -6 to 6
Outputs:
- merged: bfloat16 [16, 128, 256], P(None, ('branch', 'strip'))
- cam_grad: bfloat16 [32, 2048, 256], P(None, ('branch', 'strip'))
- lid_grad: bfloat16 [16, 128, 128], P(None, ('branch', 'strip'))
Inputs may be any that keep to these rules, and one draw needn't show every extreme that they name: For a column j of sector s = j // 64, ray_bins[j, k] lies in sector s - 1, s or s + 1 taken modulo 32, in cycle k * 16 // 118.
All inputs are finite; a program needn't handle non-finite values.
Results may differ from a plain program's by a relative error of at most 0.014.
Values may be sent and summed in bfloat16 or wider, within the bound.
A program may use at most 128 MiB of HBM per device.

v0:
```python
import jax
import jax.numpy as jnp
from jax import lax
from jax.sharding import PartitionSpec as P

BR = 16
BA = 4


def with_halo(cells, sides, width):
    for axis, dim in sides:
        count = lax.axis_size(axis)
        head = lax.slice_in_dim(cells, 0, width, axis=dim)
        tail = lax.slice_in_dim(cells, cells.shape[dim] - width, cells.shape[dim], axis=dim)
        cells = jnp.concatenate(
            [
                lax.ppermute(tail, axis, [(i, (i + 1) % count) for i in range(count)]),
                cells,
                lax.ppermute(head, axis, [((i + 1) % count, i) for i in range(count)]),
            ],
            axis=dim,
        )
    return cells


def shifted(block, axis, distance):
    devices = range(lax.axis_size(axis))
    route = [((i - distance) % len(devices), i) for i in devices]
    return lax.ppermute(block, axis, route)


def conv_taps(padded, weights, row_count, col_count):
    result = None
    for tap_index in range(9):
        down_step = tap_index // 3
        right_step = tap_index % 3
        window = padded[down_step : down_step + row_count, right_step : right_step + col_count]
        partial_value = jnp.dot(
            window.reshape(row_count * col_count, -1),
            weights[tap_index],
            preferred_element_type=jnp.float32,
        )
        result = partial_value if result is None else result + partial_value
    return result.reshape(row_count, col_count, -1)


def conv_back(padded, weights, row_count, col_count):
    result = None
    for tap_index in range(9):
        down_step = tap_index // 3
        right_step = tap_index % 3
        window = padded[
            2 - down_step : 2 - down_step + row_count, 2 - right_step : 2 - right_step + col_count
        ]
        partial_value = lax.dot_general(
            window.reshape(row_count * col_count, -1),
            weights[tap_index],
            (((1,), (1,)), ((), ())),
            preferred_element_type=jnp.float32,
        )
        result = partial_value if result is None else result + partial_value
    return result.reshape(row_count, col_count, -1)


def pad_rows(values):
    return jnp.pad(values, ((1, 1), (0, 0), (0, 0)))


def image_layer(features, weights):
    row_count, col_count = (features.shape[0], features.shape[1])
    extended = with_halo(features, ((("branch", "strip"), 1),), 1)
    return jax.nn.relu(conv_taps(pad_rows(extended), weights, row_count, col_count)).astype(
        jnp.bfloat16
    )


def slope_of(pre_act):
    gating = jax.nn.sigmoid(pre_act)
    return gating * (1.0 + pre_act * (1.0 - gating))


def local(
    image_feats,
    cam_weights,
    depth_weight,
    ray_bins,
    pillar_sums,
    pillar_counts,
    lidar_weight,
    merge_weight,
    out_cotangent,
):
    layer_total = cam_weights.shape[0]
    features = image_feats
    for layer_idx in range(layer_total):
        features = image_layer(features, cam_weights[layer_idx])
    col_count = features.shape[1]
    channels = features.shape[2]
    depth_bins = depth_weight.shape[1]
    cell_count = BR * BA
    logits = jnp.einsum("hjc,ck->hjk", features, depth_weight, preferred_element_type=jnp.float32)
    softened = jax.nn.softplus(logits) + 0.05
    totals = jnp.sum(softened, axis=2, keepdims=True)
    depth_probs = softened / totals
    probs_low = depth_probs.astype(jnp.bfloat16)
    lifted = jnp.einsum("hjk,hjc->jkc", probs_low, features, preferred_element_type=jnp.float32)
    lifted_rows = lifted.reshape(col_count * depth_bins, channels)
    flat_bins = ray_bins.reshape(-1)
    sector_count = lax.axis_size(("branch", "strip"))
    sector_index = lax.axis_index(("branch", "strip"))
    near_index = (
        flat_bins // cell_count - sector_index + 1
    ) % sector_count * cell_count + flat_bins % cell_count
    near_picker = (
        near_index[None, :] == jnp.arange(3 * cell_count, dtype=jnp.int32)[:, None]
    ).astype(jnp.float32)
    three_parts = jnp.dot(
        near_picker,
        lifted_rows,
        precision=lax.Precision.HIGHEST,
        preferred_element_type=jnp.float32,
    ).reshape(3, cell_count, channels)
    from_lower = shifted(three_parts[2], ("branch", "strip"), 1)
    from_upper = shifted(three_parts[0], ("branch", "strip"), -1)
    cam_cells = three_parts[1] + from_lower + from_upper
    cam_bev = cam_cells.reshape(BR, BA, channels).astype(jnp.bfloat16)
    occupied = (pillar_counts > 0).astype(jnp.float32)
    divisor = jnp.maximum(pillar_counts, 1).astype(jnp.float32)
    pillar_feat = (pillar_sums.astype(jnp.float32) * (occupied / divisor)[:, :, None]).astype(
        jnp.bfloat16
    )
    lidar_chans = pillar_feat.shape[2]
    grouped = pillar_feat.reshape(BR, 2, BA, 2, lidar_chans)
    lidar_sum = None
    for offset in range(4):
        window = grouped[:, offset // 2, :, offset % 2, :].reshape(BR * BA, lidar_chans)
        partial_value = jnp.dot(window, lidar_weight[offset], preferred_element_type=jnp.float32)
        lidar_sum = partial_value if lidar_sum is None else lidar_sum + partial_value
    lid_bev = jax.nn.relu(lidar_sum).reshape(BR, BA, lidar_chans).astype(jnp.bfloat16)
    merged_in = jnp.concatenate([cam_bev, lid_bev], axis=2)
    extended = with_halo(merged_in, ((("branch", "strip"), 1),), 1)
    pre_act = conv_taps(pad_rows(extended), merge_weight, BR, BA)
    merged = jax.nn.silu(pre_act).astype(jnp.bfloat16)
    grad_pre = (out_cotangent.astype(jnp.float32) * slope_of(pre_act)).astype(jnp.bfloat16)
    grad_ext = with_halo(grad_pre, ((("branch", "strip"), 1),), 1)
    grad_in = conv_back(pad_rows(grad_ext), merge_weight, BR, BA)
    lid_grad = grad_in[:, :, channels:].astype(jnp.bfloat16)
    cam_bev_grad = grad_in[:, :, :channels].astype(jnp.bfloat16).reshape(cell_count, channels)
    near_table = with_halo(
        cam_bev_grad.reshape(1, cell_count, channels), ((("branch", "strip"), 0),), 1
    )
    grad_table = near_table.reshape(3 * cell_count, channels)
    back_picker = near_picker.astype(jnp.bfloat16)
    grad_lift = (
        lax.dot_general(
            back_picker, grad_table, (((0,), (0,)), ((), ())), preferred_element_type=jnp.float32
        )
        .astype(jnp.bfloat16)
        .reshape(col_count, depth_bins, channels)
    )
    grad_probs = jnp.einsum("jkc,hjc->hjk", grad_lift, features, preferred_element_type=jnp.float32)
    grad_direct = jnp.einsum(
        "hjk,jkc->hjc", probs_low, grad_lift, preferred_element_type=jnp.float32
    )
    grad_soft = (grad_probs - jnp.sum(grad_probs * depth_probs, axis=2, keepdims=True)) / totals
    grad_logits = (grad_soft * jax.nn.sigmoid(logits)).astype(jnp.bfloat16)
    grad_depth = lax.dot_general(
        grad_logits, depth_weight, (((2,), (1,)), ((), ())), preferred_element_type=jnp.float32
    )
    cam_grad = (grad_direct + grad_depth).astype(jnp.bfloat16)
    return (merged, cam_grad, lid_grad)


def solution(mesh):
    placed = (
        P(None, ("branch", "strip"), None),
        P(),
        P(),
        P(("branch", "strip"), None),
        P(None, ("branch", "strip"), None),
        P(None, ("branch", "strip")),
        P(),
        P(),
        P(None, ("branch", "strip"), None),
    )
    return jax.shard_map(
        local,
        mesh=mesh,
        in_specs=placed,
        out_specs=(
            P(None, ("branch", "strip"), None),
            P(None, ("branch", "strip"), None),
            P(None, ("branch", "strip"), None),
        ),
        check_vma=False,
    )
```

profile of v0, /device:TPU:0, one launch (start us, length us, event | category | flops | bytes accessed | tf_op | source)
XLA Modules:
  0.0 144.8 jit_solution(3193053080447057060)
XLA Ops:
  0.7 1.7 %fusion.196 = (bf16[32,1,256]{2,1,0:T(2,128)(2,1)}, bf16[32,1,256]{2,1,0:T(2,128)(2,1)}) fusion(bf16[32,64,256]{2,1,0:T(8,128)(2,1)} %param.9), kind=kLoop, calls=%fused_computation.279 | loop fusion | bytes 65536 | tf_op jit(solution)/shard_map/slice | solution.py:14
  2.8 5.9 %collective-permute-start.1 = (bf16[32,1,256]{2,1,0:T(2,128)(2,1)}, bf16[32,1,256]{2,1,0:T(2,128)(2,1)S(1)}, u32[]{:S(2)}, u32[]{:S(2)}) collective-permute-start(bf16[32,1,256]{2,1,0:T(2,128)(2,1)} %get-tuple-element.38), channel_id=1, source_target_pairs={{1,0},{2,1},{3,2},{4,3},{5,4},{6,5},{7,6},{8,7},{9,8},{10,9},{11,1... | collective-permute-start | bytes 49160 | tf_op jit(solution)/shard_map/ppermute | solution.py:19
  12.1 1.7 %fusion.123 = f32[2048,256]{1,0:T(8,128)S(1)} fusion(bf16[2048,256]{1,0:T(8,128)(2,1)} %bitcast.252, bf16[3,9,256,256]{3,2,1,0:T(8,128)(2,1)} %param.10), kind=kOutput, calls=%fused_computation.179 | convolution fusion | flops 268435456 | bytes 3276800 | tf_op jit(solution)/shard_map/dot_general | solution.py:38
  22.3 5.3 %collective-permute-start.3 = (bf16[32,1,256]{2,1,0:T(2,128)(2,1)S(1)}, bf16[32,1,256]{2,1,0:T(2,128)(2,1)S(1)}, u32[]{:S(2)}, u32[]{:S(2)}) collective-permute-start(bf16[32,1,256]{2,1,0:T(2,128)(2,1)S(1)} %get-tuple-element.34), channel_id=1, source_target_pairs={{1,0},{2,1},{3,2},{4,3},{5,4},{6,5},{7,6},{8,7},{9,8},{10,9},{11,1... | collective-permute-start | bytes 49160 | tf_op jit(solution)/shard_map/ppermute | solution.py:19
  28.1 1.2 collective-permute-done.2
  35.4 5.6 %collective-permute-start.5 = (bf16[32,1,256]{2,1,0:T(2,128)(2,1)S(1)}, bf16[32,1,256]{2,1,0:T(2,128)(2,1)S(1)}, u32[]{:S(2)}, u32[]{:S(2)}) collective-permute-start(bf16[32,1,256]{2,1,0:T(2,128)(2,1)S(1)} %get-tuple-element.30), channel_id=1, source_target_pairs={{1,0},{2,1},{3,2},{4,3},{5,4},{6,5},{7,6},{8,7},{9,8},{10,9},{11,1... | collective-permute-start | bytes 49160 | tf_op jit(solution)/shard_map/ppermute | solution.py:19
  50.5 4.4 %fusion.43 = f32[64,118,256]{2,1,0:T(8,128)} fusion(bf16[32,64,256]{2,1,0:T(8,128)(2,1)S(1)} %bitcast.250, bf16[32,64,118]{2,1,0:T(8,128)(2,1)S(1)} %fusion.190), kind=kOutput, calls=%fused_computation.94 | convolution fusion | flops 123731968 | bytes 9265152 | tf_op jit(solution)/shard_map/hjk,hjc->jkc/dot_general | solution.py:106
  54.9 8.1 %reshape.327 = f32[7552,256]{1,0:T(8,128)} reshape(f32[64,118,256]{2,1,0:T(8,128)} %fusion.43) | data formatting | bytes 15466496 | tf_op jit(solution)/shard_map/reshape | solution.py:107
  63.1 7.2 %fusion.1 = f32[192,256]{1,0:T(8,128)S(1)} fusion(f32[7552,256]{1,0:T(8,128)} %reshape.327, s32[7552]{0:T(1024)S(1)} %fusion.177), kind=kOutput, calls=%fused_computation.4 | convolution fusion | flops 4455800832 | bytes 7960064 | tf_op jit(solution)/shard_map/dot_general | solution.py:117
  70.4 5.4 %collective-permute-start.7 = (f32[64,256]{1,0:T(8,128)S(1)}, f32[64,256]{1,0:T(8,128)S(1)}, u32[]{:S(2)}, u32[]{:S(2)}) collective-permute-start(f32[64,256]{1,0:T(8,128)S(1)} %get-tuple-element.40), channel_id=1, source_target_pairs={{1,0},{2,1},{3,2},{4,3},{5,4},{6,5},{7,6},{8,7},{9,8},{10,9},{11,1... | collective-permute-start | bytes 196616 | tf_op jit(solution)/shard_map/ppermute | solution.py:29
  75.9 1.8 %collective-permute-done.6 = f32[64,256]{1,0:T(8,128)S(1)} collective-permute-done((f32[64,256]{1,0:T(8,128)S(1)}, f32[64,256]{1,0:T(8,128)S(1)}, u32[]{:S(2)}, u32[]{:S(2)}) %collective-permute-start.6) | collective-permute-done | bytes 65568 | tf_op jit(solution)/shard_map/ppermute | solution.py:29
  77.8 5.4 %collective-permute-start.9 = (bf16[16,1,384]{2,1,0:T(2,128)(2,1)S(1)}, bf16[16,1,384]{2,1,0:T(2,128)(2,1)S(1)}, u32[]{:S(2)}, u32[]{:S(2)}) collective-permute-start(bf16[16,1,384]{2,1,0:T(2,128)(2,1)S(1)} %get-tuple-element.62), channel_id=1, source_target_pairs={{1,0},{2,1},{3,2},{4,3},{5,4},{6,5},{7,6},{8,7},{9,8},{10,9},{11,1... | collective-permute-start | bytes 36872 | tf_op jit(solution)/shard_map/ppermute | solution.py:19
  94.9 5.4 %collective-permute-start.11 = (bf16[16,1,256]{2,1,0:T(2,128)(2,1)S(1)}, bf16[16,1,256]{2,1,0:T(2,128)(2,1)S(1)}, u32[]{:S(2)}, u32[]{:S(2)}) collective-permute-start(bf16[16,1,256]{2,1,0:T(2,128)(2,1)S(1)} %get-tuple-element.66), channel_id=1, source_target_pairs={{1,0},{2,1},{3,2},{4,3},{5,4},{6,5},{7,6},{8,7},{9,8},{10,9},{11,1... | collective-permute-start | bytes 24584 | tf_op jit(solution)/shard_map/ppermute | solution.py:19
  104.3 1.1 convolution_add_fusion.23
  105.5 1.1 convolution_add_fusion.22
  106.6 1.1 fusion.32
  107.7 1.1 fusion.33
  108.9 1.1 convolution_add_fusion.19
  111.3 5.4 %collective-permute-start.13 = (bf16[1,64,256]{2,1,0:T(8,128)(2,1)S(1)}, bf16[1,64,256]{2,1,0:T(8,128)(2,1)S(1)}, u32[]{:S(2)}, u32[]{:S(2)}) collective-permute-start(bf16[1,64,256]{2,1,0:T(8,128)(2,1)S(1)} %reshape_reshape.3), channel_id=1, source_target_pairs={{1,0},{2,1},{3,2},{4,3},{5,4},{6,5},{7,6},{8,7},{9,8},{10,9},{11,1... | collective-permute-start | bytes 98312 | tf_op jit(solution)/shard_map/ppermute | solution.py:19
  118.3 3.1 %convolution_convert_fusion = bf16[7552,256]{1,0:T(8,128)(2,1)} fusion(bf16[192,256]{1,0:T(8,128)(2,1)S(1)} %bitcast.281, s32[7552]{0:T(1024)S(1)} %fusion.177), kind=kOutput, calls=%fused_computation.1 | convolution fusion | flops 748675072 | bytes 3995136 | tf_op jit(solution)/shard_map/dot_general | solution.py:155
  121.4 6.0 %reshape.349 = bf16[64,118,256]{2,1,0:T(8,128)(2,1)} reshape(bf16[7552,256]{1,0:T(8,128)(2,1)} %convolution_convert_fusion) | data formatting | bytes 7733248 | tf_op jit(solution)/shard_map/reshape | solution.py:159
  127.4 3.4 %fusion.41 = f32[64,32,118]{2,1,0:T(8,128)S(1)} fusion(bf16[64,118,256]{2,1,0:T(8,128)(2,1)} %reshape.349, bf16[32,64,256]{2,1,0:T(8,128)(2,1)S(1)} %bitcast.251), kind=kOutput, calls=%fused_computation.92 | convolution fusion | flops 123731968 | bytes 5881856 | tf_op jit(solution)/shard_map/jkc,hjc->hjk/dot_general | solution.py:161
  130.8 11.1 %fusion.21 = bf16[32,64,118]{2,1,0:T(8,128)(2,1)S(1)} fusion(f32[32,64,118]{2,1,0:T(8,128)S(1)} %get-tuple-element.68, f32[64,32,118]{2,1,0:T(8,128)S(1)} %fusion.41, f32[32,64]{1,0:T(8,128)S(1)} %fusion.49, u32[64,118]{1,0:T(8,128)S(1)} %get-tuple-element.67), kind=kOutput, calls=%fused_computation.45 | output fusion | flops 4352117 | bytes 2455040 | tf_op jit(solution)/shard_map/sub | solution.py:165
  143.3 1.6 %copy.31 = bf16[32,64,256]{2,1,0:T(8,128)(2,1)} copy(bf16[32,64,256]{2,0,1:T(8,128)(2,1)S(1)} %fusion.17) | data formatting | bytes 2097152
  (135 shorter events, 48.3 us)
Async XLA Ops:
  0.6 48.0 %copy-start = (bf16[256,118]{0,1:T(8,128)(2,1)S(1)}, bf16[256,118]{0,1:T(8,128)(2,1)}, u32[]{:S(2)}) copy-start(bf16[256,118]{0,1:T(8,128)(2,1)} %param.11) | copy-start | bytes 181252
  0.6 13.1 %copy-start.4 = (bf16[4,128,128]{2,1,0:T(8,128)(2,1)S(1)}, bf16[4,128,128]{2,1,0:T(8,128)(2,1)}, u32[]{:S(2)}) copy-start(bf16[4,128,128]{2,1,0:T(8,128)(2,1)} %param.15) | copy-start | bytes 393220
  2.3 12.7 %collective-permute-start = (bf16[32,1,256]{2,1,0:T(2,128)(2,1)}, bf16[32,1,256]{2,1,0:T(2,128)(2,1)S(1)}, u32[]{:S(2)}, u32[]{:S(2)}) collective-permute-start(bf16[32,1,256]{2,1,0:T(2,128)(2,1)} %get-tuple-element.37), channel_id=1, source_target_pairs={{0,1},{1,2},{2,3},{3,4},{4,5},{5,6},{6,7},{7,8},{8,9},{9,10},{10,1... | collective-permute-start | bytes 49160 | tf_op jit(solution)/shard_map/ppermute | solution.py:17
  2.8 12.2 %collective-permute-start.1 = (bf16[32,1,256]{2,1,0:T(2,128)(2,1)}, bf16[32,1,256]{2,1,0:T(2,128)(2,1)S(1)}, u32[]{:S(2)}, u32[]{:S(2)}) collective-permute-start(bf16[32,1,256]{2,1,0:T(2,128)(2,1)} %get-tuple-element.38), channel_id=1, source_target_pairs={{1,0},{2,1},{3,2},{4,3},{5,4},{6,5},{7,6},{8,7},{9,8},{10,9},{11,1... | collective-permute-start | bytes 49160 | tf_op jit(solution)/shard_map/ppermute | solution.py:19
  11.4 3.7 %copy-start.2 = (bf16[32,64,256]{2,1,0:T(8,128)(2,1)S(1)}, bf16[32,64,256]{2,1,0:T(8,128)(2,1)}, u32[]{:S(2)}) copy-start(bf16[32,64,256]{2,1,0:T(8,128)(2,1)} %param.9) | copy-start | bytes 3145732
  15.8 2.0 %copy-start.3 = (bf16[3,9,256,256]{3,2,1,0:T(8,128)(2,1)S(1)}, bf16[3,9,256,256]{3,2,1,0:T(8,128)(2,1)}, u32[]{:S(2)}) copy-start(bf16[3,9,256,256]{3,2,1,0:T(8,128)(2,1)} %param.10) | copy-start | bytes 10616836
  22.3 7.0 %collective-permute-start.2 = (bf16[32,1,256]{2,1,0:T(2,128)(2,1)S(1)}, bf16[32,1,256]{2,1,0:T(2,128)(2,1)S(1)}, u32[]{:S(2)}, u32[]{:S(2)}) collective-permute-start(bf16[32,1,256]{2,1,0:T(2,128)(2,1)S(1)} %get-tuple-element.33), channel_id=1, source_target_pairs={{0,1},{1,2},{2,3},{3,4},{4,5},{5,6},{6,7},{7,8},{8,9},{9,10},{10,1... | collective-permute-start | bytes 49160 | tf_op jit(solution)/shard_map/ppermute | solution.py:17
  22.3 6.9 %collective-permute-start.3 = (bf16[32,1,256]{2,1,0:T(2,128)(2,1)S(1)}, bf16[32,1,256]{2,1,0:T(2,128)(2,1)S(1)}, u32[]{:S(2)}, u32[]{:S(2)}) collective-permute-start(bf16[32,1,256]{2,1,0:T(2,128)(2,1)S(1)} %get-tuple-element.34), channel_id=1, source_target_pairs={{1,0},{2,1},{3,2},{4,3},{5,4},{6,5},{7,6},{8,7},{9,8},{10,9},{11,1... | collective-permute-start | bytes 49160 | tf_op jit(solution)/shard_map/ppermute | solution.py:19
  35.3 7.0 %collective-permute-start.4 = (bf16[32,1,256]{2,1,0:T(2,128)(2,1)S(1)}, bf16[32,1,256]{2,1,0:T(2,128)(2,1)S(1)}, u32[]{:S(2)}, u32[]{:S(2)}) collective-permute-start(bf16[32,1,256]{2,1,0:T(2,128)(2,1)S(1)} %get-tuple-element.29), channel_id=1, source_target_pairs={{0,1},{1,2},{2,3},{3,4},{4,5},{5,6},{6,7},{7,8},{8,9},{9,10},{10,1... | collective-permute-start | bytes 49160 | tf_op jit(solution)/shard_map/ppermute | solution.py:17
  35.4 7.2 %collective-permute-start.5 = (bf16[32,1,256]{2,1,0:T(2,128)(2,1)S(1)}, bf16[32,1,256]{2,1,0:T(2,128)(2,1)S(1)}, u32[]{:S(2)}, u32[]{:S(2)}) collective-permute-start(bf16[32,1,256]{2,1,0:T(2,128)(2,1)S(1)} %get-tuple-element.30), channel_id=1, source_target_pairs={{1,0},{2,1},{3,2},{4,3},{5,4},{6,5},{7,6},{8,7},{9,8},{10,9},{11,1... | collective-permute-start | bytes 49160 | tf_op jit(solution)/shard_map/ppermute | solution.py:19
  70.3 7.3 %collective-permute-start.6 = (f32[64,256]{1,0:T(8,128)S(1)}, f32[64,256]{1,0:T(8,128)S(1)}, u32[]{:S(2)}, u32[]{:S(2)}) collective-permute-start(f32[64,256]{1,0:T(8,128)S(1)} %get-tuple-element.39), channel_id=1, source_target_pairs={{31,0},{0,1},{1,2},{2,3},{3,4},{4,5},{5,6},{6,7},{7,8},{8,9},{9,10... | collective-permute-start | bytes 196616 | tf_op jit(solution)/shard_map/ppermute | solution.py:29
  70.4 7.3 %collective-permute-start.7 = (f32[64,256]{1,0:T(8,128)S(1)}, f32[64,256]{1,0:T(8,128)S(1)}, u32[]{:S(2)}, u32[]{:S(2)}) collective-permute-start(f32[64,256]{1,0:T(8,128)S(1)} %get-tuple-element.40), channel_id=1, source_target_pairs={{1,0},{2,1},{3,2},{4,3},{5,4},{6,5},{7,6},{8,7},{9,8},{10,9},{11,1... | collective-permute-start | bytes 196616 | tf_op jit(solution)/shard_map/ppermute | solution.py:29
  77.7 6.9 %collective-permute-start.8 = (bf16[16,1,384]{2,1,0:T(2,128)(2,1)S(1)}, bf16[16,1,384]{2,1,0:T(2,128)(2,1)S(1)}, u32[]{:S(2)}, u32[]{:S(2)}) collective-permute-start(bf16[16,1,384]{2,1,0:T(2,128)(2,1)S(1)} %get-tuple-element.61), channel_id=1, source_target_pairs={{0,1},{1,2},{2,3},{3,4},{4,5},{5,6},{6,7},{7,8},{8,9},{9,10},{10,1... | collective-permute-start | bytes 36872 | tf_op jit(solution)/shard_map/ppermute | solution.py:17
  77.8 7.0 %collective-permute-start.9 = (bf16[16,1,384]{2,1,0:T(2,128)(2,1)S(1)}, bf16[16,1,384]{2,1,0:T(2,128)(2,1)S(1)}, u32[]{:S(2)}, u32[]{:S(2)}) collective-permute-start(bf16[16,1,384]{2,1,0:T(2,128)(2,1)S(1)} %get-tuple-element.62), channel_id=1, source_target_pairs={{1,0},{2,1},{3,2},{4,3},{5,4},{6,5},{7,6},{8,7},{9,8},{10,9},{11,1... | collective-permute-start | bytes 36872 | tf_op jit(solution)/shard_map/ppermute | solution.py:19
  85.0 9.1 %copy-start.5 = (bf16[16,4,256]{2,1,0:T(4,128)(2,1)S(1)}, bf16[16,4,256]{2,1,0:T(4,128)(2,1)}, u32[]{:S(2)}) copy-start(bf16[16,4,256]{2,1,0:T(4,128)(2,1)} %param.17) | copy-start | bytes 98308
  94.8 6.8 %collective-permute-start.10 = (bf16[16,1,256]{2,1,0:T(2,128)(2,1)S(1)}, bf16[16,1,256]{2,1,0:T(2,128)(2,1)S(1)}, u32[]{:S(2)}, u32[]{:S(2)}) collective-permute-start(bf16[16,1,256]{2,1,0:T(2,128)(2,1)S(1)} %get-tuple-element.65), channel_id=1, source_target_pairs={{0,1},{1,2},{2,3},{3,4},{4,5},{5,6},{6,7},{7,8},{8,9},{9,10},{10,1... | collective-permute-start | bytes 24584 | tf_op jit(solution)/shard_map/ppermute | solution.py:17
  94.9 6.8 %collective-permute-start.11 = (bf16[16,1,256]{2,1,0:T(2,128)(2,1)S(1)}, bf16[16,1,256]{2,1,0:T(2,128)(2,1)S(1)}, u32[]{:S(2)}, u32[]{:S(2)}) collective-permute-start(bf16[16,1,256]{2,1,0:T(2,128)(2,1)S(1)} %get-tuple-element.66), channel_id=1, source_target_pairs={{1,0},{2,1},{3,2},{4,3},{5,4},{6,5},{7,6},{8,7},{9,8},{10,9},{11,1... | collective-permute-start | bytes 24584 | tf_op jit(solution)/shard_map/ppermute | solution.py:19
  111.2 7.0 %collective-permute-start.12 = (bf16[1,64,256]{2,1,0:T(8,128)(2,1)S(1)}, bf16[1,64,256]{2,1,0:T(8,128)(2,1)S(1)}, u32[]{:S(2)}, u32[]{:S(2)}) collective-permute-start(bf16[1,64,256]{2,1,0:T(8,128)(2,1)S(1)} %reshape_reshape.3), channel_id=1, source_target_pairs={{0,1},{1,2},{2,3},{3,4},{4,5},{5,6},{6,7},{7,8},{8,9},{9,10},{10,1... | collective-permute-start | bytes 98312 | tf_op jit(solution)/shard_map/ppermute | solution.py:17
  111.3 7.0 %collective-permute-start.13 = (bf16[1,64,256]{2,1,0:T(8,128)(2,1)S(1)}, bf16[1,64,256]{2,1,0:T(8,128)(2,1)S(1)}, u32[]{:S(2)}, u32[]{:S(2)}) collective-permute-start(bf16[1,64,256]{2,1,0:T(8,128)(2,1)S(1)} %reshape_reshape.3), channel_id=1, source_target_pairs={{1,0},{2,1},{3,2},{4,3},{5,4},{6,5},{7,6},{8,7},{9,8},{10,9},{11,1... | collective-permute-start | bytes 98312 | tf_op jit(solution)/shard_map/ppermute | solution.py:19
  130.8 11.6 %copy-start.1 = (bf16[64,118,256]{2,1,0:T(8,128)(2,1)S(1)}, bf16[64,118,256]{2,1,0:T(8,128)(2,1)}, u32[]{:S(2)}) copy-start(bf16[64,118,256]{2,1,0:T(8,128)(2,1)} %reshape.349) | copy-start | bytes 11599876
where the time goes:
time: 146 us; the launch traced here: 145 us
  matrix products  53.6 us (37%)
  starting transfers between devices  39.2 us (27%)
  local copies, waits for them, and re-layouts  25 us (17%)
  other arithmetic  19.8 us (14%)
  waiting for transfers between devices  5.86 us (4%)
    ppermute x6, starting transfers between devices, with_halo(): lax.ppermute(head, axis, [((i + 1) % count, i) for i in range(count)])  33 us
    dot_general x36, matrix products, conv_taps(): jnp.dot(window.reshape(row_count * col_count, -1), weights[tap_index], pr...  23.1 us
    sub x1, other arithmetic, local(): grad_probs - jnp.sum(grad_probs * depth_probs, axis=2, keepdims=True)  11.1 us
    dot_general x9, matrix products, conv_back(): lax.dot_general(window.reshape(row_count * col_count, -1), weights[tap_in...  10.1 us
    reshape x1, local copies, waits for them, and re-layouts, local(): lifted_rows = lifted.reshape(col_count * depth_bins, channels)  8.14 us
    dot_general x1, matrix products, local(): jnp.dot(near_picker, lifted_rows, precision=lax.Precision.HIGHEST, prefer...  7.21 us
    reshape x1, local copies, waits for them, and re-layouts, local(): grad_lift = lax.dot_general(back_picker, grad_table, (((0,), (0,)), ((),...  6.01 us
    ppermute x2, starting transfers between devices, shifted(): return lax.ppermute(block, axis, route)  5.44 us
  transfers between devices with their start and end apart: 14, of which 9 were waited for; matrix products, arithmetic and copies ran while one was open for 7% of the time, Pallas kernels for 0%

commit v1 on v0

v1 whole, which is shorter than its diff:
```python
import functools

import jax
import jax.numpy as jnp
from jax import lax
from jax.experimental import pallas as pl
from jax.experimental.pallas import tpu as pltpu
from jax.sharding import PartitionSpec as P

AXES = ("branch", "strip")
CH = 8


def rolled_sum(low, mid, high, period):
    rows = mid.shape[0]
    place = lax.broadcasted_iota(jnp.int32, mid.shape, 0) & (period - 1)
    down = jnp.where(place == 0, 0.0, pltpu.roll(low, 1, 0))
    up = jnp.where(place == period - 1, 0.0, pltpu.roll(high, rows - 1, 0))
    return mid + down + up


def conv_rows(src, starts, rows, weights, layer, height):
    taps = [
        jnp.concatenate([src[pl.ds(s + i * height, rows), :] for s in starts], axis=0)
        for i in range(3)
    ]
    x = jnp.concatenate(taps, axis=1)
    channels = taps[0].shape[1]
    z = [
        jnp.dot(
            x,
            weights[layer, 3 * dy : 3 * dy + 3].reshape(3 * channels, -1),
            preferred_element_type=jnp.float32,
        )
        for dy in range(3)
    ]
    total = rolled_sum(z[0], z[1], z[2], height)
    return jnp.maximum(total, 0.0).astype(jnp.bfloat16)


def kernel(
    n, strips, cols, height, br, ba, bins_n,
    img, cw, wd, bins, lid, cot, mw,
    merged_o, camgrad_o, lidgrad_o,
    xin, y1, y2, feats, codes, wdp, probs, slope, picker, amat, parts, sendbuf,
    rp1, rp2, rp3, rm1, rm2, rm3, win, lidwin, cotwin, table,
    local_sem, send_sem, recv_sem,
):
    me = lax.axis_index(AXES[0]) * strips + lax.axis_index(AXES[1])
    ch_rows = CH * height
    lanes = wdp.shape[1]

    def dev(d):
        t = lax.rem(me + d + n, n)
        return (t // strips, t % strips)

    barrier = pltpu.get_barrier_semaphore()
    for d in (1, 2, 3, -1, -2, -3):
        pl.semaphore_signal(
            barrier, inc=1, device_id=dev(d), device_id_type=pl.DeviceIdType.MESH
        )
    own = pltpu.make_async_copy(img, xin.at[pl.ds(3 * height, cols * height)], local_sem.at[0])
    own.start()
    own_cot = pltpu.make_async_copy(
        cot, cotwin.at[pl.ds((ba + 1) * br, ba * br)], local_sem.at[1]
    )
    own_cot.start()
    own_lid = pltpu.make_async_copy(
        lid, lidwin.at[pl.ds((ba + 2) * br, ba * br)], local_sem.at[2]
    )
    own_lid.start()

    cell = br * ba
    sh_cell, sh_ba, sh_br = cell.bit_length() - 1, ba.bit_length() - 1, br.bit_length() - 1
    raw = bins[...]
    off = (raw >> sh_cell) - me + 1
    off = jnp.where(off < 0, off + n, off)
    off = jnp.where(off >= n, off - n, off)
    in_cell = raw & (cell - 1)
    code = (((off << sh_ba) + (in_cell & (ba - 1))) << sh_br) + (in_cell >> sh_ba)
    codes[...] = jnp.full(codes.shape, -1, jnp.int32)
    codes[:, 0:bins_n] = code
    wdp[...] = jnp.zeros_like(wdp)
    wdp[:, 0:bins_n] = wd[...]
    parts[...] = jnp.zeros_like(parts)
    own.wait()

    def interior(src, dst, layer, first, shift):
        def step(i, carry):
            c = jnp.minimum(first + CH * i, cols - first - CH) + shift
            at = pl.multiple_of(c * height, height)
            dst[pl.ds(at, ch_rows), :] = conv_rows(src, [at], ch_rows, cw, layer, height)
            return carry

        lax.fori_loop(0, cols // CH, step, 0)

    interior(xin, y1, 0, 1, 2)
    own_cot.wait()
    own_lid.wait()
    pl.semaphore_wait(barrier, 6)

    messages = []

    def send(src, dst, d):
        m = len(messages)
        copy = pltpu.make_async_remote_copy(
            src_ref=src,
            dst_ref=dst,
            send_sem=send_sem.at[m],
            recv_sem=recv_sem.at[m],
            device_id=dev(d),
            device_id_type=pl.DeviceIdType.MESH,
        )
        copy.start()
        messages.append(copy)

    h3 = 3 * height
    send(xin.at[pl.ds(cols * height, h3)], xin.at[pl.ds(0, h3)], 1)
    send(xin.at[pl.ds(h3, h3)], xin.at[pl.ds((cols + 3) * height, h3)], -1)
    sec = ba * br
    send(cot, cotwin.at[pl.ds(br, sec)], 1)
    send(cot, cotwin.at[pl.ds((2 * ba + 1) * br, sec)], -1)
    send(cot.at[pl.ds(sec - br, br)], cotwin.at[pl.ds(0, br)], 2)
    send(cot.at[pl.ds(0, br)], cotwin.at[pl.ds((3 * ba + 1) * br, br)], -2)
    send(lid, lidwin.at[pl.ds(2 * br, sec)], 1)
    send(lid, lidwin.at[pl.ds((2 * ba + 2) * br, sec)], -1)
    send(lid.at[pl.ds(sec - 2 * br, 2 * br)], lidwin.at[pl.ds(0, 2 * br)], 2)
    send(lid.at[pl.ds(0, 2 * br)], lidwin.at[pl.ds((3 * ba + 2) * br, 2 * br)], -2)

    interior(y1, y2, 1, 2, 1)
    interior(y2, feats, 2, 3, 0)

    messages[0].wait_recv()
    messages[1].wait_recv()
    for layer, (src, dst, extra) in enumerate(((xin, y1, 4), (y1, y2, 2), (y2, feats, 0))):
        right = (cols + extra - 3) * height
        edge = conv_rows(src, [0, right], h3, cw, layer, height)
        dst[pl.ds(0, h3), :] = edge[:h3]
        dst[pl.ds(right, h3), :] = edge[h3:]

    groups = amat.shape[1]
    used = 3 * ba * br
    lane = lax.broadcasted_iota(jnp.int32, (ch_rows, lanes), 1)
    row_id = lax.broadcasted_iota(jnp.int32, (groups, lanes), 0)

    def lift(i, carry):
        at = pl.multiple_of(i * ch_rows, ch_rows)
        f = feats[pl.ds(at, ch_rows), :]
        logits = jnp.dot(f, wdp[...], preferred_element_type=jnp.float32)
        e = jnp.exp(-jnp.abs(logits))
        soft = jnp.maximum(logits, 0.0) + jnp.log1p(e) + 0.05
        soft = jnp.where(lane < bins_n, soft, 0.0)
        inv = 1.0 / jnp.sum(soft, axis=1, keepdims=True)
        p = soft * inv
        sig = jnp.where(logits >= 0.0, 1.0, e) / (1.0 + e)
        probs[pl.ds(at, ch_rows), :] = p
        slope[pl.ds(at, ch_rows), :] = jnp.where(lane < bins_n, sig * inv, 0.0)
        low = p.astype(jnp.bfloat16)
        rows = []
        for c in range(CH):
            j = i * CH + c
            pick = jnp.where(row_id == codes[pl.ds(j, 1), :], 1.0, 0.0).astype(jnp.bfloat16)
            picker[j] = pick
            rows.append(
                lax.dot_general(
                    low[c * height : (c + 1) * height],
                    pick,
                    (((1,), (1,)), ((), ())),
                    preferred_element_type=jnp.float32,
                )
            )
        a = jnp.concatenate(rows, axis=0).astype(jnp.bfloat16)
        amat[pl.ds(at, ch_rows), :] = a
        parts[...] += lax.dot_general(
            a, f, (((0,), (0,)), ((), ())), preferred_element_type=jnp.float32
        )
        return carry

    lax.fori_loop(0, cols // CH, lift, 0)

    mine = parts[0:used, :]
    sendbuf[...] = mine.astype(jnp.bfloat16)
    n1, n2, n3 = (2 * ba + 2) * br, (ba + 2) * br, 2 * br
    send(sendbuf.at[pl.ds(used - n1, n1)], rp1, 1)
    send(sendbuf.at[pl.ds(0, n1)], rm1, -1)
    send(sendbuf.at[pl.ds(used - n2, n2)], rp2, 2)
    send(sendbuf.at[pl.ds(0, n2)], rm2, -2)
    send(sendbuf.at[pl.ds(used - n3, n3)], rp3, 3)
    send(sendbuf.at[pl.ds(0, n3)], rm3, -3)
    total = win.shape[0]
    win[...] = jnp.zeros_like(win)
    win[pl.ds(2 * br, used), :] = mine
    for copy in messages[2:]:
        copy.wait_recv()
    for got, size in ((rp1, n1), (rp2, n2), (rp3, n3)):
        win[pl.ds(0, size), :] += got[...].astype(jnp.float32)
    for got, size in ((rm1, n1), (rm2, n2), (rm3, n3)):
        win[pl.ds(total - size, size), :] += got[...].astype(jnp.float32)

    cam = win[...].astype(jnp.bfloat16)
    channels = cam.shape[1]
    joined = jnp.concatenate([cam, lidwin[...]], axis=1)
    cc = joined.shape[1]
    act_rows = total - 2 * br
    x = jnp.concatenate([joined[i * br : i * br + act_rows] for i in range(3)], axis=1)
    z = [
        jnp.dot(
            x,
            mw[3 * dy : 3 * dy + 3].reshape(3 * cc, -1),
            preferred_element_type=jnp.float32,
        )
        for dy in range(3)
    ]
    act = rolled_sum(z[0], z[1], z[2], br)
    gate = 1.0 / (1.0 + jnp.exp(-act))
    begin = (ba + 1) * br
    merged_o[...] = (act * gate)[begin : begin + sec].astype(jnp.bfloat16)
    grad_pre = (
        cotwin[...].astype(jnp.float32) * (gate * (1.0 + act * (1.0 - gate)))
    ).astype(jnp.bfloat16)
    y = []
    for dy in range(3):
        acc = None
        for i in range(3):
            term = lax.dot_general(
                grad_pre[(2 - i) * br : (2 - i) * br + used],
                mw[3 * dy + i],
                (((1,), (1,)), ((), ())),
                preferred_element_type=jnp.float32,
            )
            acc = term if acc is None else acc + term
        y.append(acc)
    grad_in = rolled_sum(y[2], y[1], y[0], br)
    table[...] = jnp.zeros_like(table)
    table[0:used, :] = grad_in[:, :channels].astype(jnp.bfloat16)
    lidgrad_o[...] = grad_in[sec : 2 * sec, channels:].astype(jnp.bfloat16)

    def back(i, carry):
        at = pl.multiple_of(i * ch_rows, ch_rows)
        f = feats[pl.ds(at, ch_rows), :]
        tab = table[...]
        g = lax.dot_general(
            f, tab, (((1,), (1,)), ((), ())), preferred_element_type=jnp.float32
        ).astype(jnp.bfloat16)
        direct = jnp.dot(amat[pl.ds(at, ch_rows), :], tab, preferred_element_type=jnp.float32)
        gp = jnp.concatenate(
            [
                jnp.dot(
                    g[c * height : (c + 1) * height],
                    picker[i * CH + c],
                    preferred_element_type=jnp.float32,
                )
                for c in range(CH)
            ],
            axis=0,
        )
        mean = jnp.sum(gp * probs[pl.ds(at, ch_rows), :], axis=1, keepdims=True)
        gl = ((gp - mean) * slope[pl.ds(at, ch_rows), :]).astype(jnp.bfloat16)
        depth = lax.dot_general(
            gl, wdp[...], (((1,), (1,)), ((), ())), preferred_element_type=jnp.float32
        )
        camgrad_o[pl.ds(at, ch_rows), :] = (direct + depth).astype(jnp.bfloat16)
        return carry

    lax.fori_loop(0, cols // CH, back, 0)
    for copy in messages:
        copy.wait_send()


def local(
    n, strips,
    image_feats, cam_weights, depth_weight, ray_bins, pillar_sums, pillar_counts,
    lidar_weight, merge_weight, out_cotangent,
):
    height, cols, channels = image_feats.shape
    br, ba, cf = out_cotangent.shape
    bins_n = depth_weight.shape[1]
    cl = pillar_sums.shape[2]
    lanes = -(-bins_n // 128) * 128
    groups = -(-3 * ba * br // 128) * 128
    used = 3 * ba * br
    total = (3 * ba + 4) * br
    sec = ba * br
    bf, f32 = jnp.bfloat16, jnp.float32

    img = image_feats.transpose(1, 0, 2).reshape(cols * height, channels)
    cot = out_cotangent.transpose(1, 0, 2).reshape(sec, cf)
    occupied = (pillar_counts > 0).astype(f32)
    divisor = jnp.maximum(pillar_counts, 1).astype(f32)
    pillar_feat = (pillar_sums.astype(f32) * (occupied / divisor)[:, :, None]).astype(bf)
    taps = pillar_feat.reshape(br, 2, ba, 2, cl).transpose(2, 0, 1, 3, 4).reshape(sec, 4 * cl)
    lid = jnp.dot(taps, lidar_weight.reshape(4 * cl, cl), preferred_element_type=f32)
    lid = jax.nn.relu(lid).astype(bf)

    vm = pl.BlockSpec(memory_space=pltpu.VMEM)
    n1, n2, n3 = (2 * ba + 2) * br, (ba + 2) * br, 2 * br
    merged, cam_grad, lid_grad = pl.pallas_call(
        functools.partial(kernel, n, strips, cols, height, br, ba, bins_n),
        out_shape=(
            jax.ShapeDtypeStruct((sec, cf), bf),
            jax.ShapeDtypeStruct((cols * height, channels), bf),
            jax.ShapeDtypeStruct((sec, cl), bf),
        ),
        in_specs=[vm] * 7,
        out_specs=(vm, vm, vm),
        scratch_shapes=[
            pltpu.VMEM(((cols + 6) * height, channels), bf),
            pltpu.VMEM(((cols + 4) * height, channels), bf),
            pltpu.VMEM(((cols + 2) * height, channels), bf),
            pltpu.VMEM((cols * height, channels), bf),
            pltpu.VMEM((cols, lanes), jnp.int32),
            pltpu.VMEM((channels, lanes), bf),
            pltpu.VMEM((cols * height, lanes), f32),
            pltpu.VMEM((cols * height, lanes), f32),
            pltpu.VMEM((cols, groups, lanes), bf),
            pltpu.VMEM((cols * height, groups), bf),
            pltpu.VMEM((groups, channels), f32),
            pltpu.VMEM((used, channels), bf),
            pltpu.VMEM((n1, channels), bf),
            pltpu.VMEM((n2, channels), bf),
            pltpu.VMEM((n3, channels), bf),
            pltpu.VMEM((n1, channels), bf),
            pltpu.VMEM((n2, channels), bf),
            pltpu.VMEM((n3, channels), bf),
            pltpu.VMEM((total, channels), f32),
            pltpu.VMEM((total, cl), bf),
            pltpu.VMEM((total - 2 * br, cf), bf),
            pltpu.VMEM((groups, channels), bf),
            pltpu.SemaphoreType.DMA((3,)),
            pltpu.SemaphoreType.DMA((16,)),
            pltpu.SemaphoreType.DMA((16,)),
        ],
        compiler_params=pltpu.CompilerParams(
            collective_id=0, has_side_effects=True, vmem_limit_bytes=58 * 1024 * 1024
        ),
        name="bev",
    )(img, cam_weights, depth_weight, ray_bins, lid, cot, merge_weight)
    return (
        merged.reshape(ba, br, cf).transpose(1, 0, 2),
        cam_grad.reshape(cols, height, channels).transpose(1, 0, 2),
        lid_grad.reshape(ba, br, cl).transpose(1, 0, 2),
    )


def solution(mesh):
    strips = mesh.shape["strip"]
    n = mesh.shape["branch"] * strips
    placed = (
        P(None, AXES, None),
        P(),
        P(),
        P(AXES, None),
        P(None, AXES, None),
        P(None, AXES),
        P(),
        P(),
        P(None, AXES, None),
    )
    return jax.shard_map(
        functools.partial(local, n, strips),
        mesh=mesh,
        in_specs=placed,
        out_specs=(P(None, AXES, None),) * 3,
        check_vma=False,
    )
```

time: 146 us -> 56.2 us (0.38)
  matrix products: 53.6 us -> 0.77 us
  Pallas kernels: 0 us -> 40.3 us
  starting transfers between devices: 39.2 us -> 0 us
  other arithmetic: 19.8 us -> 1.63 us
  local copies, waits for them, and re-layouts: 25 us -> 12.3 us
  waiting for transfers between devices: 5.86 us -> 0 us
    dot_general x56 -> x1, matrix products: 53.6 us -> 0.77 us  [local(): jnp.dot(taps, lidar_weight.reshape(4 * cl, cl), preferred_element_type=f32)]
    pallas_call x0 -> x1, Pallas kernels: none -> 40.3 us  [local(): pl.pallas_call(functools.partial(kernel, n, strips, cols, height, br, ba,...]
    ppermute x14 -> x0, starting transfers between devices: 39.2 us -> none  [the longest x6 33 us: with_halo(): lax.ppermute(head, axis, [((i + 1) % count, i) for i in range(count)])]
    sub x1 -> x0, other arithmetic: 11.1 us -> none  [local(): grad_probs - jnp.sum(grad_probs * depth_probs, axis=2, keepdims=True)]
    reshape x21 -> x5, local copies, waits for them, and re-layouts: 15.3 us -> 5.58 us  [the longest x1 2.78 us: local(): cam_grad.reshape(cols, height, channels).transpose(1, 0, 2)]
    slice x13 -> x0, local copies, waits for them, and re-layouts: 6.02 us -> none  [the longest x4 2.8 us: conv_taps(): padded[down_step:down_step + row_count, right_step:right_step + col_count]]
    ppermute x14 -> x0, waiting for transfers between devices: 5.86 us -> none  [the longest x6 3.63 us: with_halo(): lax.ppermute(tail, axis, [(i, (i + 1) % count) for i in range(count)])]
    concatenate x12 -> x0, other arithmetic: 4.81 us -> none  [the longest x11 4.77 us: with_halo(): jnp.concatenate([lax.ppermute(tail, axis, [(i, (i + 1) % count) for i in...]
  transfers between devices with their start and end apart: 14 -> 0, of which waited for: 9 -> 0; matrix products, arithmetic and copies ran while one was open for 7% -> 0% of each run, Pallas kernels for 0% -> 0%
where the time goes in v1:
time: 56.2 us; the launch traced here: 55.7 us
  Pallas kernels  40.3 us (72%)
  local copies, waits for them, and re-layouts  12.3 us (22%)
  other arithmetic  1.63 us (3%)
  matrix products  0.77 us (1%)
  between operations  0.67 us (1%)
    pallas_call x1, Pallas kernels, local(): pl.pallas_call(functools.partial(kernel, n, strips, cols, height, br, ba,...  40.3 us
    transpose x1, local copies, waits for them, and re-layouts, local(): img = image_feats.transpose(1, 0, 2).reshape(cols * height, channels)  2.78 us
    reshape x1, local copies, waits for them, and re-layouts, local(): cam_grad.reshape(cols, height, channels).transpose(1, 0, 2)  2.78 us
    unnamed x3, local copies, waits for them, and re-layouts  2.47 us
    reshape x1, local copies, waits for them, and re-layouts, local(): merged.reshape(ba, br, cf).transpose(1, 0, 2)  1.39 us
    transpose x1, local copies, waits for them, and re-layouts, local(): cot = out_cotangent.transpose(1, 0, 2).reshape(sec, cf)  1.38 us
    reshape x1, local copies, waits for them, and re-layouts, local(): lid_grad.reshape(ba, br, cl).transpose(1, 0, 2)  1.33 us

profile of v1, /device:TPU:0, one launch (start us, length us, event | category | flops | bytes accessed | tf_op | source)
XLA Modules:
  0.0 55.7 jit_solution(18047216061512963262)
XLA Ops:
  0.6 0.0 copy-start
  0.6 0.9 %copy-done = bf16[4,128,128]{2,1,0:T(8,128)(2,1)S(1)} copy-done((bf16[4,128,128]{2,1,0:T(8,128)(2,1)S(1)}, bf16[4,128,128]{2,1,0:T(8,128)(2,1)}, u32[]{:S(2)}) %copy-start) | copy-done | bytes 131096
  1.5 0.7 %convert_divide_fusion = f32[32,8]{0,1:T(8,128)S(1)} fusion(s32[32,8]{0,1:T(8,128)} %param.14), kind=kLoop, calls=%fused_computation.7 | loop fusion | flops 1280 | bytes 2048 | tf_op jit(solution)/shard_map/div | solution.py:290
  2.2 0.1 copy.20
  2.3 1.4 %copy.22 = bf16[4,16,256]{2,1,0:T(8,128)(2,1)} copy(bf16[4,16,256]{2,0,1:T(4,128)(2,1)} %bitcast.31) | data formatting | bytes 65536 | tf_op jit(solution)/shard_map/transpose | solution.py:287
  3.7 0.9 %multiply_convert_fusion = bf16[32,8,128]{2,1,0:T(8,128)(2,1)S(1)} fusion(bf16[32,8,128]{2,1,0:T(8,128)(2,1)} %param.13, f32[32,8]{1,0:T(8,128)S(1)} %copy.20), kind=kLoop, calls=%fused_computation.3 | loop fusion | flops 98304 | bytes 132096 | tf_op jit(solution)/shard_map/convert_element_type | solution.py:290
  4.7 0.8 %fusion.lid = bf16[64,128]{1,0:T(8,128)(2,1)} fusion(bf16[64,512]{1,0:T(8,128)(2,1)S(1)} %reshape.33, bf16[512,128]{1,0:T(8,128)(2,1)S(1)} %bitcast.23), kind=kOutput, calls=%fused_computation.1 | convolution fusion | flops 8404992 | bytes 212992 | tf_op jit(solution)/shard_map/dot_general | solution.py:292
  5.5 1.6 %copy.23.wd = bf16[256,118]{1,0:T(8,128)(2,1)} copy(bf16[256,118]{0,1:T(8,128)(2,1)} %param.11) | data formatting | bytes 120832 | tf_op args[2]
  7.1 2.8 %copy.19 = bf16[64,32,256]{2,1,0:T(8,128)(2,1)} copy(bf16[64,32,256]{2,0,1:T(8,128)(2,1)} %bitcast.25) | data formatting | bytes 2097152 | tf_op jit(solution)/shard_map/transpose | solution.py:286
  9.8 40.3 %bev.1 = (bf16[64,256]{1,0:T(8,128)(2,1)}, bf16[2048,256]{1,0:T(8,128)(2,1)}, bf16[64,128]{1,0:T(8,128)(2,1)}) custom-call(bf16[2048,256]{1,0:T(8,128)(2,1)} %bitcast.24, bf16[3,9,256,256]{3,2,1,0:T(8,128)(2,1)} %cw.1, bf16[256,118]{1,0:T(8,128)(2,1)} %copy.23.wd, s32[64,118]{1,0:T(8,128)} %bins.1, bf16[64,128]{1,0:T(8,128)(2,1)} %fusion.lid, ...), custom_call_target="tpu_custom_call" | custom-call | tf_op jit(solution)/shard_map/bev/pallas_call | solution.py:297
  50.2 1.4 %copy.33 = bf16[4,16,256]{2,0,1:T(4,128)(2,1)} copy(bf16[4,16,256]{2,1,0:T(8,128)(2,1)} %bitcast.33) | data formatting | bytes 65536 | tf_op jit(solution)/shard_map/reshape | solution.py:339
  51.6 2.8 %copy.31 = bf16[64,32,256]{2,0,1:T(8,128)(2,1)} copy(bf16[64,32,256]{2,1,0:T(8,128)(2,1)} %bitcast.27) | data formatting | bytes 2097152 | tf_op jit(solution)/shard_map/reshape | solution.py:340
  54.3 1.3 %copy.34 = bf16[4,16,128]{2,0,1:T(4,128)(2,1)} copy(bf16[4,16,128]{2,1,0:T(8,128)(2,1)} %bitcast.35) | data formatting | bytes 32768 | tf_op jit(solution)/shard_map/reshape | solution.py:341
  (2 shorter events, 0.1 us)
Async XLA Ops:
  0.6 0.9 %copy-start = (bf16[4,128,128]{2,1,0:T(8,128)(2,1)S(1)}, bf16[4,128,128]{2,1,0:T(8,128)(2,1)}, u32[]{:S(2)}) copy-start(bf16[4,128,128]{2,1,0:T(8,128)(2,1)} %param.15) | copy-start | bytes 393220

commit v2 on v1

--- a/solution.py
+++ b/solution.py
@@ -38,17 +38,23 @@
     return jnp.maximum(total, 0.0).astype(jnp.bfloat16)
 
 
+def one_hot_rows(rows, sources, source_of):
+    p = lax.broadcasted_iota(jnp.int32, (rows, sources), 0)
+    q = lax.broadcasted_iota(jnp.int32, (rows, sources), 1)
+    return jnp.where(source_of(p) == q, 1.0, 0.0).astype(jnp.bfloat16)
+
+
 def kernel(
     n, strips, cols, height, br, ba, bins_n,
-    img, cw, wd, bins, lid, cot, mw,
+    img, cw_hbm, wd, bins, pillars, counts, lw, cot, mw_hbm,
     merged_o, camgrad_o, lidgrad_o,
-    xin, y1, y2, feats, codes, wdp, probs, slope, picker, amat, parts, sendbuf,
+    cw, mw, xin, y1, y2, feats, codes, wdp, probs, slope, picker, amat, parts, sendbuf,
     rp1, rp2, rp3, rm1, rm2, rm3, win, lidwin, cotwin, table,
     local_sem, send_sem, recv_sem,
 ):
     me = lax.axis_index(AXES[0]) * strips + lax.axis_index(AXES[1])
     ch_rows = CH * height
-    lanes = wdp.shape[1]
+    lanes = wdp.shape[0]
 
     def dev(d):
         t = lax.rem(me + d + n, n)
@@ -59,16 +65,49 @@
         pl.semaphore_signal(
             barrier, inc=1, device_id=dev(d), device_id_type=pl.DeviceIdType.MESH
         )
-    own = pltpu.make_async_copy(img, xin.at[pl.ds(3 * height, cols * height)], local_sem.at[0])
-    own.start()
-    own_cot = pltpu.make_async_copy(
-        cot, cotwin.at[pl.ds((ba + 1) * br, ba * br)], local_sem.at[1]
-    )
-    own_cot.start()
-    own_lid = pltpu.make_async_copy(
-        lid, lidwin.at[pl.ds((ba + 2) * br, ba * br)], local_sem.at[2]
-    )
-    own_lid.start()
+    layers = cw.shape[0]
+    fetches = [
+        pltpu.make_async_copy(cw_hbm.at[k], cw.at[k], local_sem.at[k]) for k in range(layers)
+    ]
+    fetches.append(pltpu.make_async_copy(mw_hbm, mw, local_sem.at[layers]))
+    for copy in fetches:
+        copy.start()
+
+    sh_h, sh_ch = height.bit_length() - 1, CH.bit_length() - 1
+    to_cols = one_hot_rows(
+        ch_rows, ch_rows, lambda p: ((p & (height - 1)) << sh_ch) + (p >> sh_h)
+    )
+    for i in range(cols // CH):
+        block = img[:, i * CH : (i + 1) * CH, :].astype(jnp.float32)
+        block = block.reshape(ch_rows, -1).astype(jnp.bfloat16)
+        turned = jnp.dot(to_cols, block, preferred_element_type=jnp.float32)
+        xin[pl.ds((3 + i * CH) * height, ch_rows), :] = turned.astype(jnp.bfloat16)
+
+    sec = ba * br
+    cot_own, lid_own = (ba + 1) * br, (ba + 2) * br
+    cot_f = cot[...].astype(jnp.float32)
+    for a in range(ba):
+        cotwin[pl.ds(cot_own + a * br, br), :] = cot_f[:, a, :].astype(jnp.bfloat16)
+    points = counts[...]
+    scale = (points > 0).astype(jnp.float32) / jnp.maximum(points, 1).astype(jnp.float32)
+    pil = pillars[...].astype(jnp.float32)
+    pil = jnp.concatenate(
+        [pil[k] * scale[:, k : k + 1] for k in range(2 * br)], axis=0
+    ).astype(jnp.bfloat16)
+    lb, la = br.bit_length() - 1, ba.bit_length() - 1
+
+    def pillar_row(p):
+        r, a, uv = p & (br - 1), (p >> lb) & (ba - 1), p >> (lb + la)
+        return ((2 * r + (uv >> 1)) << (la + 1)) + 2 * a + (uv & 1)
+
+    gathered = jnp.dot(
+        one_hot_rows(4 * sec, 4 * sec, pillar_row), pil, preferred_element_type=jnp.float32
+    ).astype(jnp.bfloat16)
+    taps = jnp.concatenate([gathered[k * sec : (k + 1) * sec] for k in range(4)], axis=1)
+    lid = jnp.dot(
+        taps, lw[...].reshape(taps.shape[1], -1), preferred_element_type=jnp.float32
+    )
+    lidwin[pl.ds(lid_own, sec), :] = jnp.maximum(lid, 0.0).astype(jnp.bfloat16)
 
     cell = br * ba
     sh_cell, sh_ba, sh_br = cell.bit_length() - 1, ba.bit_length() - 1, br.bit_length() - 1
@@ -81,9 +120,9 @@
     codes[...] = jnp.full(codes.shape, -1, jnp.int32)
     codes[:, 0:bins_n] = code
     wdp[...] = jnp.zeros_like(wdp)
-    wdp[:, 0:bins_n] = wd[...]
+    wdp[0:bins_n, :] = wd[...]
     parts[...] = jnp.zeros_like(parts)
-    own.wait()
+    fetches[0].wait()
 
     def interior(src, dst, layer, first, shift):
         def step(i, carry):
@@ -95,8 +134,6 @@
         lax.fori_loop(0, cols // CH, step, 0)
 
     interior(xin, y1, 0, 1, 2)
-    own_cot.wait()
-    own_lid.wait()
     pl.semaphore_wait(barrier, 6)
 
     messages = []
@@ -117,17 +154,17 @@
     h3 = 3 * height
     send(xin.at[pl.ds(cols * height, h3)], xin.at[pl.ds(0, h3)], 1)
     send(xin.at[pl.ds(h3, h3)], xin.at[pl.ds((cols + 3) * height, h3)], -1)
-    sec = ba * br
-    send(cot, cotwin.at[pl.ds(br, sec)], 1)
-    send(cot, cotwin.at[pl.ds((2 * ba + 1) * br, sec)], -1)
-    send(cot.at[pl.ds(sec - br, br)], cotwin.at[pl.ds(0, br)], 2)
-    send(cot.at[pl.ds(0, br)], cotwin.at[pl.ds((3 * ba + 1) * br, br)], -2)
-    send(lid, lidwin.at[pl.ds(2 * br, sec)], 1)
-    send(lid, lidwin.at[pl.ds((2 * ba + 2) * br, sec)], -1)
-    send(lid.at[pl.ds(sec - 2 * br, 2 * br)], lidwin.at[pl.ds(0, 2 * br)], 2)
-    send(lid.at[pl.ds(0, 2 * br)], lidwin.at[pl.ds((3 * ba + 2) * br, 2 * br)], -2)
-
+    for window, start, edge in ((cotwin, cot_own, br), (lidwin, lid_own, 2 * br)):
+        mine = window.at[pl.ds(start, sec)]
+        send(mine, window.at[pl.ds(edge, sec)], 1)
+        send(mine, window.at[pl.ds(start + sec, sec)], -1)
+        last = window.at[pl.ds(start + sec - edge, edge)]
+        send(last, window.at[pl.ds(0, edge)], 2)
+        send(window.at[pl.ds(start, edge)], window.at[pl.ds(start + 2 * sec, edge)], -2)
+
+    fetches[1].wait()
     interior(y1, y2, 1, 2, 1)
+    fetches[2].wait()
     interior(y2, feats, 2, 3, 0)
 
     messages[0].wait_recv()
@@ -146,7 +183,9 @@
     def lift(i, carry):
         at = pl.multiple_of(i * ch_rows, ch_rows)
         f = feats[pl.ds(at, ch_rows), :]
-        logits = jnp.dot(f, wdp[...], preferred_element_type=jnp.float32)
+        logits = lax.dot_general(
+            f, wdp[...], (((1,), (1,)), ((), ())), preferred_element_type=jnp.float32
+        )
         e = jnp.exp(-jnp.abs(logits))
         soft = jnp.maximum(logits, 0.0) + jnp.log1p(e) + 0.05
         soft = jnp.where(lane < bins_n, soft, 0.0)
@@ -190,6 +229,7 @@
     total = win.shape[0]
     win[...] = jnp.zeros_like(win)
     win[pl.ds(2 * br, used), :] = mine
+    fetches[layers].wait()
     for copy in messages[2:]:
         copy.wait_recv()
     for got, size in ((rp1, n1), (rp2, n2), (rp3, n3)):
@@ -213,8 +253,10 @@
     ]
     act = rolled_sum(z[0], z[1], z[2], br)
     gate = 1.0 / (1.0 + jnp.exp(-act))
-    begin = (ba + 1) * br
-    merged_o[...] = (act * gate)[begin : begin + sec].astype(jnp.bfloat16)
+    merged = (act * gate)[cot_own : cot_own + sec]
+    merged_o[...] = jnp.stack(
+        [merged[a * br : (a + 1) * br] for a in range(ba)], axis=1
+    ).astype(jnp.bfloat16)
     grad_pre = (
         cotwin[...].astype(jnp.float32) * (gate * (1.0 + act * (1.0 - gate)))
     ).astype(jnp.bfloat16)
@@ -233,7 +275,13 @@
     grad_in = rolled_sum(y[2], y[1], y[0], br)
     table[...] = jnp.zeros_like(table)
     table[0:used, :] = grad_in[:, :channels].astype(jnp.bfloat16)
-    lidgrad_o[...] = grad_in[sec : 2 * sec, channels:].astype(jnp.bfloat16)
+    lid_grad = grad_in[sec : 2 * sec, channels:]
+    lidgrad_o[...] = jnp.stack(
+        [lid_grad[a * br : (a + 1) * br] for a in range(ba)], axis=1
+    ).astype(jnp.bfloat16)
+    to_rows = one_hot_rows(
+        ch_rows, ch_rows, lambda p: ((p & (CH - 1)) << sh_h) + (p >> sh_ch)
+    )
 
     def back(i, carry):
         at = pl.multiple_of(i * ch_rows, ch_rows)
@@ -256,10 +304,12 @@
         )
         mean = jnp.sum(gp * probs[pl.ds(at, ch_rows), :], axis=1, keepdims=True)
         gl = ((gp - mean) * slope[pl.ds(at, ch_rows), :]).astype(jnp.bfloat16)
-        depth = lax.dot_general(
-            gl, wdp[...], (((1,), (1,)), ((), ())), preferred_element_type=jnp.float32
-        )
-        camgrad_o[pl.ds(at, ch_rows), :] = (direct + depth).astype(jnp.bfloat16)
+        depth = jnp.dot(gl, wdp[...], preferred_element_type=jnp.float32)
+        block = (direct + depth).astype(jnp.bfloat16)
+        turned = jnp.dot(to_rows, block, preferred_element_type=jnp.float32)
+        camgrad_o[:, pl.ds(pl.multiple_of(i * CH, CH), CH), :] = turned.reshape(
+            height, CH, -1
+        ).astype(jnp.bfloat16)
         return carry
 
     lax.fori_loop(0, cols // CH, back, 0)
@@ -280,36 +330,29 @@
     groups = -(-3 * ba * br // 128) * 128
     used = 3 * ba * br
     total = (3 * ba + 4) * br
-    sec = ba * br
     bf, f32 = jnp.bfloat16, jnp.float32
 
-    img = image_feats.transpose(1, 0, 2).reshape(cols * height, channels)
-    cot = out_cotangent.transpose(1, 0, 2).reshape(sec, cf)
-    occupied = (pillar_counts > 0).astype(f32)
-    divisor = jnp.maximum(pillar_counts, 1).astype(f32)
-    pillar_feat = (pillar_sums.astype(f32) * (occupied / divisor)[:, :, None]).astype(bf)
-    taps = pillar_feat.reshape(br, 2, ba, 2, cl).transpose(2, 0, 1, 3, 4).reshape(sec, 4 * cl)
-    lid = jnp.dot(taps, lidar_weight.reshape(4 * cl, cl), preferred_element_type=f32)
-    lid = jax.nn.relu(lid).astype(bf)
-
     vm = pl.BlockSpec(memory_space=pltpu.VMEM)
+    hbm = pl.BlockSpec(memory_space=pl.ANY)
     n1, n2, n3 = (2 * ba + 2) * br, (ba + 2) * br, 2 * br
-    merged, cam_grad, lid_grad = pl.pallas_call(
+    return pl.pallas_call(
         functools.partial(kernel, n, strips, cols, height, br, ba, bins_n),
         out_shape=(
-            jax.ShapeDtypeStruct((sec, cf), bf),
-            jax.ShapeDtypeStruct((cols * height, channels), bf),
-            jax.ShapeDtypeStruct((sec, cl), bf),
+            jax.ShapeDtypeStruct((br, ba, cf), bf),
+            jax.ShapeDtypeStruct((height, cols, channels), bf),
+            jax.ShapeDtypeStruct((br, ba, cl), bf),
         ),
-        in_specs=[vm] * 7,
+        in_specs=[vm, hbm, vm, vm, vm, vm, vm, vm, hbm],
         out_specs=(vm, vm, vm),
         scratch_shapes=[
+            pltpu.VMEM(cam_weights.shape, bf),
+            pltpu.VMEM(merge_weight.shape, bf),
             pltpu.VMEM(((cols + 6) * height, channels), bf),
             pltpu.VMEM(((cols + 4) * height, channels), bf),
             pltpu.VMEM(((cols + 2) * height, channels), bf),
             pltpu.VMEM((cols * height, channels), bf),
             pltpu.VMEM((cols, lanes), jnp.int32),
-            pltpu.VMEM((channels, lanes), bf),
+            pltpu.VMEM((lanes, channels), bf),
             pltpu.VMEM((cols * height, lanes), f32),
             pltpu.VMEM((cols * height, lanes), f32),
             pltpu.VMEM((cols, groups, lanes), bf),
@@ -326,7 +369,7 @@
             pltpu.VMEM((total, cl), bf),
             pltpu.VMEM((total - 2 * br, cf), bf),
             pltpu.VMEM((groups, channels), bf),
-            pltpu.SemaphoreType.DMA((3,)),
+            pltpu.SemaphoreType.DMA((cam_weights.shape[0] + 1,)),
             pltpu.SemaphoreType.DMA((16,)),
             pltpu.SemaphoreType.DMA((16,)),
         ],
@@ -334,11 +377,9 @@
             collective_id=0, has_side_effects=True, vmem_limit_bytes=58 * 1024 * 1024
         ),
         name="bev",
-    )(img, cam_weights, depth_weight, ray_bins, lid, cot, merge_weight)
-    return (
-        merged.reshape(ba, br, cf).transpose(1, 0, 2),
-        cam_grad.reshape(cols, height, channels).transpose(1, 0, 2),
-        lid_grad.reshape(ba, br, cl).transpose(1, 0, 2),
+    )(
+        image_feats, cam_weights, depth_weight.T, ray_bins, pillar_sums, pillar_counts.T,
+        lidar_weight, out_cotangent, merge_weight,
     )
 
 

time: 56.2 us -> 47.9 us (0.85)
  local copies, waits for them, and re-layouts: 12.3 us -> 5.02 us
  other arithmetic: 1.63 us -> 0 us
  Pallas kernels: 40.3 us -> 41.9 us
  matrix products: 0.77 us -> 0 us
    reshape x5 -> x0, local copies, waits for them, and re-layouts: 5.58 us -> none  [the longest x1 2.78 us: local(): cam_grad.reshape(cols, height, channels).transpose(1, 0, 2)]
    transpose x2 -> x0, local copies, waits for them, and re-layouts: 4.16 us -> none  [the longest x1 2.78 us: local(): img = image_feats.transpose(1, 0, 2).reshape(cols * height, channels)]
    unnamed x3, local copies, waits for them, and re-layouts: 2.47 us -> 5.02 us
    pallas_call x1, Pallas kernels: 40.3 us -> 41.9 us  [local(): pl.pallas_call(functools.partial(kernel, n, strips, cols, height, br, ba,...]
    convert_element_type x1 -> x0, other arithmetic: 0.94 us -> none  [local(): (pillar_sums.astype(f32) * (occupied / divisor)[:, :, None]).astype(bf)]
    dot_general x1 -> x0, matrix products: 0.77 us -> none  [local(): jnp.dot(taps, lidar_weight.reshape(4 * cl, cl), preferred_element_type=f32)]
    div x1 -> x0, other arithmetic: 0.69 us -> none  [local(): occupied / divisor]
where the time goes in v2:
time: 47.9 us; the launch traced here: 47.6 us
  Pallas kernels  41.9 us (87%)
  local copies, waits for them, and re-layouts  5.02 us (10%)
  between operations  0.64 us (1%)
    pallas_call x1, Pallas kernels, local(): pl.pallas_call(functools.partial(kernel, n, strips, cols, height, br, ba,...  41.9 us
    unnamed x3, local copies, waits for them, and re-layouts  5.02 us

profile of v2, /device:TPU:0, one launch (start us, length us, event | category | flops | bytes accessed | tf_op | source)
XLA Modules:
  0.0 47.6 jit_solution(11421955452875667729)
XLA Ops:
  0.6 41.9 %bev.1 = (bf16[16,4,256]{2,1,0:T(4,128)(2,1)}, bf16[32,64,256]{2,1,0:T(8,128)(2,1)}, bf16[16,4,128]{2,1,0:T(4,128)(2,1)}) custom-call(bf16[32,64,256]{2,1,0:T(8,128)(2,1)} %img.1, bf16[3,9,256,256]{3,2,1,0:T(8,128)(2,1)} %cw_hbm.1, bf16[118,256]{1,0:T(8,128)(2,1)} %bitcast.2, s32[64,118]{1,0:T(8,128)} %bins.1, bf16[32,8,128]{2,1,0:T(8,128)(2,1)} %pillars.1, ...), custom_call_target="tpu_custom_call" | custom-call | tf_op jit(solution)/shard_map/bev/pallas_call | solution.py:338
  42.6 1.4 %copy.15 = bf16[16,4,256]{2,1,0:T(4,128)(2,1)} copy(bf16[16,4,256]{2,1,0:T(4,128)(2,1)} %get-tuple-element.6) | data formatting | bytes 65536
  43.9 2.3 %copy.16 = bf16[32,64,256]{2,1,0:T(8,128)(2,1)} copy(bf16[32,64,256]{2,1,0:T(8,128)(2,1)} %get-tuple-element.7) | data formatting | bytes 2097152
  46.2 1.3 %copy.17 = bf16[16,4,128]{2,1,0:T(4,128)(2,1)} copy(bf16[16,4,128]{2,1,0:T(4,128)(2,1)} %get-tuple-element.8) | data formatting | bytes 32768

commit v3 on v2

--- a/solution.py
+++ b/solution.py
@@ -44,13 +44,25 @@
     return jnp.where(source_of(p) == q, 1.0, 0.0).astype(jnp.bfloat16)
 
 
+def row_numbers(shape):
+    return lax.broadcasted_iota(jnp.int32, shape, 0).astype(jnp.float32).astype(jnp.bfloat16)
+
+
+def pick_of(row_id, codes, j):
+    groups, lanes = row_id.shape
+    code = jnp.broadcast_to(codes[pl.ds(j, 1), :], (16, lanes)).astype(jnp.bfloat16)
+    code = jnp.concatenate([code] * (groups // 16), axis=0)
+    one, zero = jnp.ones((), jnp.bfloat16), jnp.zeros((), jnp.bfloat16)
+    return jnp.where(row_id[...] == code, one, zero)
+
+
 def kernel(
     n, strips, cols, height, br, ba, bins_n,
     img, cw_hbm, wd, bins, pillars, counts, lw, cot, mw_hbm,
-    merged_o, camgrad_o, lidgrad_o,
-    cw, mw, xin, y1, y2, feats, codes, wdp, probs, slope, picker, amat, parts, sendbuf,
-    rp1, rp2, rp3, rm1, rm2, rm3, win, lidwin, cotwin, table,
-    local_sem, send_sem, recv_sem,
+    merged_o, lidgrad_o, table, codes, feats_o, amat_o, probs_o, slope_o,
+    cw, mw, xin, y1, y2, feats, wdp, probs, slope, low, row_id, amat, parts, sendbuf,
+    rp1, rp2, rp3, rm1, rm2, rm3, win, lidwin, cotwin,
+    local_sem, out_sem, send_sem, recv_sem,
 ):
     me = lax.axis_index(AXES[0]) * strips + lax.axis_index(AXES[1])
     ch_rows = CH * height
@@ -117,8 +129,9 @@
     off = jnp.where(off >= n, off - n, off)
     in_cell = raw & (cell - 1)
     code = (((off << sh_ba) + (in_cell & (ba - 1))) << sh_br) + (in_cell >> sh_ba)
-    codes[...] = jnp.full(codes.shape, -1, jnp.int32)
-    codes[:, 0:bins_n] = code
+    codes[...] = jnp.full(codes.shape, -1.0, jnp.float32)
+    codes[:, 0:bins_n] = code.astype(jnp.float32)
+    row_id[...] = row_numbers(row_id.shape)
     wdp[...] = jnp.zeros_like(wdp)
     wdp[0:bins_n, :] = wd[...]
     parts[...] = jnp.zeros_like(parts)
@@ -175,12 +188,17 @@
         dst[pl.ds(0, h3), :] = edge[:h3]
         dst[pl.ds(right, h3), :] = edge[h3:]
 
-    groups = amat.shape[1]
+    outs = []
+
+    def write(src, dst):
+        copy = pltpu.make_async_copy(src, dst, out_sem.at[len(outs)])
+        copy.start()
+        outs.append(copy)
+
     used = 3 * ba * br
     lane = lax.broadcasted_iota(jnp.int32, (ch_rows, lanes), 1)
-    row_id = lax.broadcasted_iota(jnp.int32, (groups, lanes), 0)
-
-    def lift(i, carry):
+
+    def soften(i, carry):
         at = pl.multiple_of(i * ch_rows, ch_rows)
         f = feats[pl.ds(at, ch_rows), :]
         logits = lax.dot_general(
@@ -194,28 +212,37 @@
         sig = jnp.where(logits >= 0.0, 1.0, e) / (1.0 + e)
         probs[pl.ds(at, ch_rows), :] = p
         slope[pl.ds(at, ch_rows), :] = jnp.where(lane < bins_n, sig * inv, 0.0)
-        low = p.astype(jnp.bfloat16)
-        rows = []
+        low[pl.ds(at, ch_rows), :] = p.astype(jnp.bfloat16)
+        return carry
+
+    lax.fori_loop(0, cols // CH, soften, 0)
+
+    def lift(i, carry):
         for c in range(CH):
             j = i * CH + c
-            pick = jnp.where(row_id == codes[pl.ds(j, 1), :], 1.0, 0.0).astype(jnp.bfloat16)
-            picker[j] = pick
-            rows.append(
-                lax.dot_general(
-                    low[c * height : (c + 1) * height],
-                    pick,
-                    (((1,), (1,)), ((), ())),
-                    preferred_element_type=jnp.float32,
-                )
+            at = pl.multiple_of(j * height, height)
+            a = lax.dot_general(
+                low[pl.ds(at, height), :],
+                pick_of(row_id, codes, j),
+                (((1,), (1,)), ((), ())),
+                preferred_element_type=jnp.float32,
             )
-        a = jnp.concatenate(rows, axis=0).astype(jnp.bfloat16)
-        amat[pl.ds(at, ch_rows), :] = a
+            amat[pl.ds(at, height), :] = a.astype(jnp.bfloat16)
+        return carry
+
+    lax.fori_loop(0, cols // CH, lift, 0)
+
+    def gather(i, carry):
+        at = pl.multiple_of(i * 2 * ch_rows, 2 * ch_rows)
         parts[...] += lax.dot_general(
-            a, f, (((0,), (0,)), ((), ())), preferred_element_type=jnp.float32
+            amat[pl.ds(at, 2 * ch_rows), :],
+            feats[pl.ds(at, 2 * ch_rows), :],
+            (((0,), (0,)), ((), ())),
+            preferred_element_type=jnp.float32,
         )
         return carry
 
-    lax.fori_loop(0, cols // CH, lift, 0)
+    lax.fori_loop(0, cols // (2 * CH), gather, 0)
 
     mine = parts[0:used, :]
     sendbuf[...] = mine.astype(jnp.bfloat16)
@@ -226,6 +253,10 @@
     send(sendbuf.at[pl.ds(0, n2)], rm2, -2)
     send(sendbuf.at[pl.ds(used - n3, n3)], rp3, 3)
     send(sendbuf.at[pl.ds(0, n3)], rm3, -3)
+    write(feats, feats_o)
+    write(amat, amat_o)
+    write(probs, probs_o)
+    write(slope, slope_o)
     total = win.shape[0]
     win[...] = jnp.zeros_like(win)
     win[pl.ds(2 * br, used), :] = mine
@@ -279,42 +310,60 @@
     lidgrad_o[...] = jnp.stack(
         [lid_grad[a * br : (a + 1) * br] for a in range(ba)], axis=1
     ).astype(jnp.bfloat16)
+    for copy in messages:
+        copy.wait_send()
+    for copy in outs:
+        copy.wait()
+
+
+def back_kernel(
+    height, bins_n,
+    feats, amat, probs, slope, codes, table, wd, merged, lid_grad,
+    camgrad_o, merged_o, lidgrad_o,
+    wdp, row_id,
+):
+    step = pl.program_id(0)
+    ch_rows = CH * height
+    sh_h, sh_ch = height.bit_length() - 1, CH.bit_length() - 1
+
+    @pl.when(step == 0)
+    def _():
+        merged_o[...] = merged[...]
+        lidgrad_o[...] = lid_grad[...]
+        wdp[...] = jnp.zeros_like(wdp)
+        wdp[0:bins_n, :] = wd[...]
+        row_id[...] = row_numbers(row_id.shape)
+
     to_rows = one_hot_rows(
         ch_rows, ch_rows, lambda p: ((p & (CH - 1)) << sh_h) + (p >> sh_ch)
     )
-
-    def back(i, carry):
-        at = pl.multiple_of(i * ch_rows, ch_rows)
-        f = feats[pl.ds(at, ch_rows), :]
-        tab = table[...]
+    chunks = feats.shape[0] // ch_rows
+    tab = table[...]
+    for k in range(chunks):
+        rows = pl.ds(k * ch_rows, ch_rows)
         g = lax.dot_general(
-            f, tab, (((1,), (1,)), ((), ())), preferred_element_type=jnp.float32
+            feats[rows, :], tab, (((1,), (1,)), ((), ())), preferred_element_type=jnp.float32
         ).astype(jnp.bfloat16)
-        direct = jnp.dot(amat[pl.ds(at, ch_rows), :], tab, preferred_element_type=jnp.float32)
+        direct = jnp.dot(amat[rows, :], tab, preferred_element_type=jnp.float32)
         gp = jnp.concatenate(
             [
                 jnp.dot(
                     g[c * height : (c + 1) * height],
-                    picker[i * CH + c],
+                    pick_of(row_id, codes, (step * chunks + k) * CH + c),
                     preferred_element_type=jnp.float32,
                 )
                 for c in range(CH)
             ],
             axis=0,
         )
-        mean = jnp.sum(gp * probs[pl.ds(at, ch_rows), :], axis=1, keepdims=True)
-        gl = ((gp - mean) * slope[pl.ds(at, ch_rows), :]).astype(jnp.bfloat16)
+        mean = jnp.sum(gp * probs[rows, :], axis=1, keepdims=True)
+        gl = ((gp - mean) * slope[rows, :]).astype(jnp.bfloat16)
         depth = jnp.dot(gl, wdp[...], preferred_element_type=jnp.float32)
         block = (direct + depth).astype(jnp.bfloat16)
         turned = jnp.dot(to_rows, block, preferred_element_type=jnp.float32)
-        camgrad_o[:, pl.ds(pl.multiple_of(i * CH, CH), CH), :] = turned.reshape(
-            height, CH, -1
-        ).astype(jnp.bfloat16)
-        return carry
-
-    lax.fori_loop(0, cols // CH, back, 0)
-    for copy in messages:
-        copy.wait_send()
+        camgrad_o[:, k * CH : (k + 1) * CH, :] = turned.reshape(height, CH, -1).astype(
+            jnp.bfloat16
+        )
 
 
 def local(
@@ -335,15 +384,21 @@
     vm = pl.BlockSpec(memory_space=pltpu.VMEM)
     hbm = pl.BlockSpec(memory_space=pl.ANY)
     n1, n2, n3 = (2 * ba + 2) * br, (ba + 2) * br, 2 * br
-    return pl.pallas_call(
+    rows = cols * height
+    merged, lid_grad, table, codes, feats, amat, probs, slope = pl.pallas_call(
         functools.partial(kernel, n, strips, cols, height, br, ba, bins_n),
         out_shape=(
             jax.ShapeDtypeStruct((br, ba, cf), bf),
-            jax.ShapeDtypeStruct((height, cols, channels), bf),
             jax.ShapeDtypeStruct((br, ba, cl), bf),
+            jax.ShapeDtypeStruct((groups, channels), bf),
+            jax.ShapeDtypeStruct((cols, lanes), f32),
+            jax.ShapeDtypeStruct((rows, channels), bf),
+            jax.ShapeDtypeStruct((rows, groups), bf),
+            jax.ShapeDtypeStruct((rows, lanes), f32),
+            jax.ShapeDtypeStruct((rows, lanes), f32),
         ),
         in_specs=[vm, hbm, vm, vm, vm, vm, vm, vm, hbm],
-        out_specs=(vm, vm, vm),
+        out_specs=(vm,) * 4 + (hbm,) * 4,
         scratch_shapes=[
             pltpu.VMEM(cam_weights.shape, bf),
             pltpu.VMEM(merge_weight.shape, bf),
@@ -351,11 +406,11 @@
             pltpu.VMEM(((cols + 4) * height, channels), bf),
             pltpu.VMEM(((cols + 2) * height, channels), bf),
             pltpu.VMEM((cols * height, channels), bf),
-            pltpu.VMEM((cols, lanes), jnp.int32),
             pltpu.VMEM((lanes, channels), bf),
             pltpu.VMEM((cols * height, lanes), f32),
             pltpu.VMEM((cols * height, lanes), f32),
-            pltpu.VMEM((cols, groups, lanes), bf),
+            pltpu.VMEM((cols * height, lanes), bf),
+            pltpu.VMEM((groups, lanes), bf),
             pltpu.VMEM((cols * height, groups), bf),
             pltpu.VMEM((groups, channels), f32),
             pltpu.VMEM((used, channels), bf),
@@ -368,8 +423,8 @@
             pltpu.VMEM((total, channels), f32),
             pltpu.VMEM((total, cl), bf),
             pltpu.VMEM((total - 2 * br, cf), bf),
-            pltpu.VMEM((groups, channels), bf),
             pltpu.SemaphoreType.DMA((cam_weights.shape[0] + 1,)),
+            pltpu.SemaphoreType.DMA((4,)),
             pltpu.SemaphoreType.DMA((16,)),
             pltpu.SemaphoreType.DMA((16,)),
         ],
@@ -381,6 +436,36 @@
         image_feats, cam_weights, depth_weight.T, ray_bins, pillar_sums, pillar_counts.T,
         lidar_weight, out_cotangent, merge_weight,
     )
+    steps = cols // (2 * CH)
+
+    def rowed(width):
+        return pl.BlockSpec((rows // steps, width), lambda i: (i, 0))
+
+    def whole(*shape):
+        return pl.BlockSpec(shape, lambda i: (0,) * len(shape))
+
+    cam_grad, merged, lid_grad = pl.pallas_call(
+        functools.partial(back_kernel, height, bins_n),
+        grid=(steps,),
+        out_shape=(
+            jax.ShapeDtypeStruct((height, cols, channels), bf),
+            jax.ShapeDtypeStruct((br, ba, cf), bf),
+            jax.ShapeDtypeStruct((br, ba, cl), bf),
+        ),
+        in_specs=[
+            rowed(channels), rowed(groups), rowed(lanes), rowed(lanes),
+            whole(cols, lanes), whole(groups, channels), whole(bins_n, channels),
+            whole(br, ba, cf), whole(br, ba, cl),
+        ],
+        out_specs=(
+            pl.BlockSpec((height, cols // steps, channels), lambda i: (0, i, 0)),
+            whole(br, ba, cf),
+            whole(br, ba, cl),
+        ),
+        scratch_shapes=[pltpu.VMEM((lanes, channels), bf), pltpu.VMEM((groups, lanes), bf)],
+        name="back",
+    )(feats, amat, probs, slope, codes, table, depth_weight.T, merged, lid_grad)
+    return merged, cam_grad, lid_grad
 
 
 def solution(mesh):

time: 47.9 us -> 43.2 us (0.902)
  local copies, waits for them, and re-layouts: 5.02 us -> 0 us
  Pallas kernels: 41.9 us -> 42.4 us
    pallas_call x0 -> x1, Pallas kernels: none -> 8.29 us  [local(): pl.pallas_call(functools.partial(back_kernel, height, bins_n), grid=(step...]
    pallas_call x1, Pallas kernels: 41.9 us -> 34.1 us  [local(): pl.pallas_call(functools.partial(kernel, n, strips, cols, height, br, ba,...]
    unnamed x3 -> x0, local copies, waits for them, and re-layouts: 5.02 us -> none
where the time goes in v3:
time: 43.2 us; the launch traced here: 43 us
  Pallas kernels  42.4 us (98%)
  between operations  0.64 us (1%)
    pallas_call x1, Pallas kernels, local(): pl.pallas_call(functools.partial(kernel, n, strips, cols, height, br, ba,...  34.1 us
    pallas_call x1, Pallas kernels, local(): pl.pallas_call(functools.partial(back_kernel, height, bins_n), grid=(step...  8.29 us

profile of v3, /device:TPU:0, one launch (start us, length us, event | category | flops | bytes accessed | tf_op | source)
XLA Modules:
  0.0 43.0 jit_solution(17596936881886123415)
XLA Ops:
  0.6 34.1 %bev.1 = (bf16[16,4,256]{2,1,0:T(4,128)(2,1)}, bf16[16,4,128]{2,1,0:T(4,128)(2,1)}, bf16[256,256]{1,0:T(8,128)(2,1)}, f32[64,128]{1,0:T(8,128)}, bf16[2048,256]{...) custom-call(bf16[32,64,256]{2,1,0:T(8,128)(2,1)} %img.1, ...), custom_call_target="tpu_custom_call" | custom-call | tf_op jit(solution)/shard_map/bev/pallas_call | solution.py:388
  34.8 8.3 %back.1 = (bf16[32,64,256]{2,1,0:T(8,128)(2,1)}, bf16[16,4,256]{2,1,0:T(4,128)(2,1)}, bf16[16,4,128]{2,1,0:T(4,128)(2,1)}) custom-call(bf16[2048,256]{1,0:T(8,128)(2,1)} %get-tuple-element.14.feats, bf16[2048,256]{1,0:T(8,128)(2,1)} %get-tuple-element.15.amat, f32[2048,128]{1,0:T(8,128)} %get-tuple-element.16.probs, f32[2048,128]{1,0:T(8,128)} %get-tuple-element.17.slope, ...), custom_call_target="tpu_custom_call" | custom-call | tf_op jit(solution)/shard_map/back/pallas_call | solution.py:447

commit v4 on v3

--- a/solution.py
+++ b/solution.py
@@ -9,6 +9,7 @@
 
 AXES = ("branch", "strip")
 CH = 8
+BLOCK = 16
 
 
 def rolled_sum(low, mid, high, period):
@@ -56,11 +57,20 @@
     return jnp.where(row_id[...] == code, one, zero)
 
 
+def block_turn():
+    shift = BLOCK.bit_length() - 1
+    return one_hot_rows(
+        BLOCK * BLOCK,
+        BLOCK * BLOCK,
+        lambda p: ((p & (BLOCK - 1)) << shift) + (p >> shift),
+    )
+
+
 def kernel(
     n, strips, cols, height, br, ba, bins_n,
     img, cw_hbm, wd, bins, pillars, counts, lw, cot, mw_hbm,
     merged_o, lidgrad_o, table, codes, feats_o, amat_o, probs_o, slope_o,
-    cw, mw, xin, y1, y2, feats, wdp, probs, slope, low, row_id, amat, parts, sendbuf,
+    cw, mw, xin, y1, y2, feats, wdp, probs, slope, sums, low, row_id, amat, parts, sendbuf,
     rp1, rp2, rp3, rm1, rm2, rm3, win, lidwin, cotwin,
     local_sem, out_sem, send_sem, recv_sem,
 ):
@@ -85,15 +95,15 @@
     for copy in fetches:
         copy.start()
 
-    sh_h, sh_ch = height.bit_length() - 1, CH.bit_length() - 1
-    to_cols = one_hot_rows(
-        ch_rows, ch_rows, lambda p: ((p & (height - 1)) << sh_ch) + (p >> sh_h)
-    )
-    for i in range(cols // CH):
-        block = img[:, i * CH : (i + 1) * CH, :].astype(jnp.float32)
-        block = block.reshape(ch_rows, -1).astype(jnp.bfloat16)
-        turned = jnp.dot(to_cols, block, preferred_element_type=jnp.float32)
-        xin[pl.ds((3 + i * CH) * height, ch_rows), :] = turned.astype(jnp.bfloat16)
+    turn = block_turn()
+    for j0 in range(0, cols, BLOCK):
+        for h0 in range(0, height, BLOCK):
+            block = img[h0 : h0 + BLOCK, j0 : j0 + BLOCK, :].reshape(BLOCK * BLOCK, -1)
+            turned = jnp.dot(turn, block, preferred_element_type=jnp.float32)
+            turned = turned.astype(jnp.bfloat16)
+            for c in range(BLOCK):
+                at = (3 + j0 + c) * height + h0
+                xin[pl.ds(at, BLOCK), :] = turned[c * BLOCK : (c + 1) * BLOCK]
 
     sec = ba * br
     cot_own, lid_own = (ba + 1) * br, (ba + 2) * br
@@ -209,9 +219,9 @@
         soft = jnp.where(lane < bins_n, soft, 0.0)
         inv = 1.0 / jnp.sum(soft, axis=1, keepdims=True)
         p = soft * inv
-        sig = jnp.where(logits >= 0.0, 1.0, e) / (1.0 + e)
         probs[pl.ds(at, ch_rows), :] = p
-        slope[pl.ds(at, ch_rows), :] = jnp.where(lane < bins_n, sig * inv, 0.0)
+        slope[pl.ds(at, ch_rows), :] = logits
+        sums[pl.ds(at, ch_rows), :] = inv
         low[pl.ds(at, ch_rows), :] = p.astype(jnp.bfloat16)
         return carry
 
@@ -256,33 +266,45 @@
     write(feats, feats_o)
     write(amat, amat_o)
     write(probs, probs_o)
+
+    def bend(i, carry):
+        at = pl.multiple_of(i * ch_rows, ch_rows)
+        sig = jax.nn.sigmoid(slope[pl.ds(at, ch_rows), :]) * sums[pl.ds(at, ch_rows), :]
+        slope[pl.ds(at, ch_rows), :] = jnp.where(lane < bins_n, sig, 0.0)
+        return carry
+
+    lax.fori_loop(0, cols // CH, bend, 0)
+    for copy in messages[2:10]:
+        copy.wait_recv()
+    fetches[layers].wait()
+    channels = feats.shape[1]
+    total = win.shape[0]
+    act_rows = total - 2 * br
+
+    def merge(source, lo, hi):
+        x = jnp.concatenate([source[i * br : i * br + act_rows] for i in range(3)], axis=1)
+        z = [
+            jnp.dot(
+                x,
+                mw[3 * dy : 3 * dy + 3, lo:hi, :].reshape(3 * (hi - lo), -1),
+                preferred_element_type=jnp.float32,
+            )
+            for dy in range(3)
+        ]
+        return rolled_sum(z[0], z[1], z[2], br)
+
+    lid_act = merge(lidwin[...], channels, mw.shape[1])
     write(slope, slope_o)
-    total = win.shape[0]
     win[...] = jnp.zeros_like(win)
     win[pl.ds(2 * br, used), :] = mine
-    fetches[layers].wait()
-    for copy in messages[2:]:
+    for copy in messages[10:]:
         copy.wait_recv()
     for got, size in ((rp1, n1), (rp2, n2), (rp3, n3)):
         win[pl.ds(0, size), :] += got[...].astype(jnp.float32)
     for got, size in ((rm1, n1), (rm2, n2), (rm3, n3)):
         win[pl.ds(total - size, size), :] += got[...].astype(jnp.float32)
 
-    cam = win[...].astype(jnp.bfloat16)
-    channels = cam.shape[1]
-    joined = jnp.concatenate([cam, lidwin[...]], axis=1)
-    cc = joined.shape[1]
-    act_rows = total - 2 * br
-    x = jnp.concatenate([joined[i * br : i * br + act_rows] for i in range(3)], axis=1)
-    z = [
-        jnp.dot(
-            x,
-            mw[3 * dy : 3 * dy + 3].reshape(3 * cc, -1),
-            preferred_element_type=jnp.float32,
-        )
-        for dy in range(3)
-    ]
-    act = rolled_sum(z[0], z[1], z[2], br)
+    act = lid_act + merge(win[...].astype(jnp.bfloat16), 0, channels)
     gate = 1.0 / (1.0 + jnp.exp(-act))
     merged = (act * gate)[cot_own : cot_own + sec]
     merged_o[...] = jnp.stack(
@@ -291,22 +313,24 @@
     grad_pre = (
         cotwin[...].astype(jnp.float32) * (gate * (1.0 + act * (1.0 - gate)))
     ).astype(jnp.bfloat16)
-    y = []
-    for dy in range(3):
-        acc = None
-        for i in range(3):
-            term = lax.dot_general(
-                grad_pre[(2 - i) * br : (2 - i) * br + used],
-                mw[3 * dy + i],
-                (((1,), (1,)), ((), ())),
-                preferred_element_type=jnp.float32,
-            )
-            acc = term if acc is None else acc + term
-        y.append(acc)
-    grad_in = rolled_sum(y[2], y[1], y[0], br)
-    table[...] = jnp.zeros_like(table)
-    table[0:used, :] = grad_in[:, :channels].astype(jnp.bfloat16)
-    lid_grad = grad_in[sec : 2 * sec, channels:]
+
+    def merge_back(first, rows, lo, hi):
+        y = []
+        for dy in range(3):
+            acc = None
+            for i in range(3):
+                term = lax.dot_general(
+                    grad_pre[first + (2 - i) * br : first + (2 - i) * br + rows],
+                    mw[3 * dy + i, lo:hi, :],
+                    (((1,), (1,)), ((), ())),
+                    preferred_element_type=jnp.float32,
+                )
+                acc = term if acc is None else acc + term
+            y.append(acc)
+        return rolled_sum(y[2], y[1], y[0], br)
+
+    table[...] = merge_back(0, used, 0, channels).astype(jnp.bfloat16)
+    lid_grad = merge_back(sec, sec, channels, mw.shape[1])
     lidgrad_o[...] = jnp.stack(
         [lid_grad[a * br : (a + 1) * br] for a in range(ba)], axis=1
     ).astype(jnp.bfloat16)
@@ -324,7 +348,6 @@
 ):
     step = pl.program_id(0)
     ch_rows = CH * height
-    sh_h, sh_ch = height.bit_length() - 1, CH.bit_length() - 1
 
     @pl.when(step == 0)
     def _():
@@ -334,9 +357,8 @@
         wdp[0:bins_n, :] = wd[...]
         row_id[...] = row_numbers(row_id.shape)
 
-    to_rows = one_hot_rows(
-        ch_rows, ch_rows, lambda p: ((p & (CH - 1)) << sh_h) + (p >> sh_ch)
-    )
+    turn = block_turn()
+    blocks = []
     chunks = feats.shape[0] // ch_rows
     tab = table[...]
     for k in range(chunks):
@@ -359,10 +381,15 @@
         mean = jnp.sum(gp * probs[rows, :], axis=1, keepdims=True)
         gl = ((gp - mean) * slope[rows, :]).astype(jnp.bfloat16)
         depth = jnp.dot(gl, wdp[...], preferred_element_type=jnp.float32)
-        block = (direct + depth).astype(jnp.bfloat16)
-        turned = jnp.dot(to_rows, block, preferred_element_type=jnp.float32)
-        camgrad_o[:, k * CH : (k + 1) * CH, :] = turned.reshape(height, CH, -1).astype(
-            jnp.bfloat16
+        blocks.append((direct + depth).astype(jnp.bfloat16))
+    block = jnp.concatenate(blocks, axis=0)
+    for h0 in range(0, height, BLOCK):
+        part = jnp.concatenate(
+            [block[c * height + h0 : c * height + h0 + BLOCK] for c in range(BLOCK)], axis=0
+        )
+        turned = jnp.dot(turn, part, preferred_element_type=jnp.float32)
+        camgrad_o[h0 : h0 + BLOCK, :, :] = turned.astype(jnp.bfloat16).reshape(
+            BLOCK, BLOCK, -1
         )
 
 
@@ -376,8 +403,7 @@
     bins_n = depth_weight.shape[1]
     cl = pillar_sums.shape[2]
     lanes = -(-bins_n // 128) * 128
-    groups = -(-3 * ba * br // 128) * 128
-    used = 3 * ba * br
+    used = groups = 3 * ba * br
     total = (3 * ba + 4) * br
     bf, f32 = jnp.bfloat16, jnp.float32
 
@@ -409,6 +435,7 @@
             pltpu.VMEM((lanes, channels), bf),
             pltpu.VMEM((cols * height, lanes), f32),
             pltpu.VMEM((cols * height, lanes), f32),
+            pltpu.VMEM((cols * height, 1), f32),
             pltpu.VMEM((cols * height, lanes), bf),
             pltpu.VMEM((groups, lanes), bf),
             pltpu.VMEM((cols * height, groups), bf),
@@ -436,7 +463,7 @@
         image_feats, cam_weights, depth_weight.T, ray_bins, pillar_sums, pillar_counts.T,
         lidar_weight, out_cotangent, merge_weight,
     )
-    steps = cols // (2 * CH)
+    steps = cols // BLOCK
 
     def rowed(width):
         return pl.BlockSpec((rows // steps, width), lambda i: (i, 0))

time: 43.2 us -> 42.6 us (0.986)
  Pallas kernels: 42.4 us -> 41.8 us
    pallas_call x1, Pallas kernels: 8.29 us -> 7.64 us  [local(): pl.pallas_call(functools.partial(back_kernel, height, bins_n), grid=(step...]
where the time goes in v4:
time: 42.6 us; the launch traced here: 42.4 us
  Pallas kernels  41.8 us (98%)
  between operations  0.64 us (2%)
    pallas_call x1, Pallas kernels, local(): pl.pallas_call(functools.partial(kernel, n, strips, cols, height, br, ba,...  34.1 us
    pallas_call x1, Pallas kernels, local(): pl.pallas_call(functools.partial(back_kernel, height, bins_n), grid=(step...  7.64 us

profile of v4, /device:TPU:0, one launch (start us, length us, event | category | flops | bytes accessed | tf_op | source)
XLA Modules:
  0.0 42.4 jit_solution(3020083057049038263)
XLA Ops:
  0.6 34.1 %bev.1 = (bf16[16,4,256]{2,1,0:T(4,128)(2,1)}, bf16[16,4,128]{2,1,0:T(4,128)(2,1)}, bf16[192,256]{1,0:T(8,128)(2,1)}, f32[64,128]{1,0:T(8,128)}, bf16[2048,256]{...) custom-call(bf16[32,64,256]{2,1,0:T(8,128)(2,1)} %img.1, ...), custom_call_target="tpu_custom_call" | custom-call | tf_op jit(solution)/shard_map/bev/pallas_call | solution.py:414
  34.8 7.6 %back.1 = (bf16[32,64,256]{2,1,0:T(8,128)(2,1)}, bf16[16,4,256]{2,1,0:T(4,128)(2,1)}, bf16[16,4,128]{2,1,0:T(4,128)(2,1)}) custom-call(bf16[2048,256]{1,0:T(8,128)(2,1)} %get-tuple-element.14.feats, bf16[2048,192]{1,0:T(8,128)(2,1)} %get-tuple-element.15.amat, f32[2048,128]{1,0:T(8,128)} %get-tuple-element.16.probs, f32[2048,128]{1,0:T(8,128)} %get-tuple-element.17.slope, ...), custom_call_target="tpu_custom_call" | custom-call | tf_op jit(solution)/shard_map/back/pallas_call | solution.py:474

commit v5 on v4

--- a/solution.py
+++ b/solution.py
@@ -20,9 +20,9 @@
     return mid + down + up
 
 
-def conv_rows(src, starts, rows, weights, layer, height):
+def conv_rows(src, pieces, weights, layer, height):
     taps = [
-        jnp.concatenate([src[pl.ds(s + i * height, rows), :] for s in starts], axis=0)
+        jnp.concatenate([src[pl.ds(s + i * height, rows), :] for s, rows in pieces], axis=0)
         for i in range(3)
     ]
     x = jnp.concatenate(taps, axis=1)
@@ -68,9 +68,9 @@
 
 def kernel(
     n, strips, cols, height, br, ba, bins_n,
-    img, cw_hbm, wd, bins, pillars, counts, lw, cot, mw_hbm,
+    img_hbm, cw_hbm, wd, bins, pillars, counts, lw, cot, mw_hbm,
     merged_o, lidgrad_o, table, codes, feats_o, amat_o, probs_o, slope_o,
-    cw, mw, xin, y1, y2, feats, wdp, probs, slope, sums, low, row_id, amat, parts, sendbuf,
+    img, cw, mw, xin, y1, y2, feats, wdp, probs, slope, sums, low, row_id, amat, parts, sendbuf,
     rp1, rp2, rp3, rm1, rm2, rm3, win, lidwin, cotwin,
     local_sem, out_sem, send_sem, recv_sem,
 ):
@@ -88,22 +88,14 @@
             barrier, inc=1, device_id=dev(d), device_id_type=pl.DeviceIdType.MESH
         )
     layers = cw.shape[0]
+    image = pltpu.make_async_copy(img_hbm, img, local_sem.at[layers + 1])
+    image.start()
     fetches = [
         pltpu.make_async_copy(cw_hbm.at[k], cw.at[k], local_sem.at[k]) for k in range(layers)
     ]
     fetches.append(pltpu.make_async_copy(mw_hbm, mw, local_sem.at[layers]))
     for copy in fetches:
         copy.start()
-
-    turn = block_turn()
-    for j0 in range(0, cols, BLOCK):
-        for h0 in range(0, height, BLOCK):
-            block = img[h0 : h0 + BLOCK, j0 : j0 + BLOCK, :].reshape(BLOCK * BLOCK, -1)
-            turned = jnp.dot(turn, block, preferred_element_type=jnp.float32)
-            turned = turned.astype(jnp.bfloat16)
-            for c in range(BLOCK):
-                at = (3 + j0 + c) * height + h0
-                xin[pl.ds(at, BLOCK), :] = turned[c * BLOCK : (c + 1) * BLOCK]
 
     sec = ba * br
     cot_own, lid_own = (ba + 1) * br, (ba + 2) * br
@@ -145,18 +137,29 @@
     wdp[...] = jnp.zeros_like(wdp)
     wdp[0:bins_n, :] = wd[...]
     parts[...] = jnp.zeros_like(parts)
+    image.wait()
+    turn = block_turn()
+    for j0 in range(0, cols, BLOCK):
+        for h0 in range(0, height, BLOCK):
+            block = img[h0 : h0 + BLOCK, j0 : j0 + BLOCK, :].reshape(BLOCK * BLOCK, -1)
+            turned = jnp.dot(turn, block, preferred_element_type=jnp.float32)
+            turned = turned.astype(jnp.bfloat16)
+            for c in range(BLOCK):
+                at = (3 + j0 + c) * height + h0
+                xin[pl.ds(at, BLOCK), :] = turned[c * BLOCK : (c + 1) * BLOCK]
     fetches[0].wait()
 
-    def interior(src, dst, layer, first, shift):
+    def interior(src, dst, layer, first, shift, count):
         def step(i, carry):
             c = jnp.minimum(first + CH * i, cols - first - CH) + shift
             at = pl.multiple_of(c * height, height)
-            dst[pl.ds(at, ch_rows), :] = conv_rows(src, [at], ch_rows, cw, layer, height)
+            dst[pl.ds(at, ch_rows), :] = conv_rows(src, [(at, ch_rows)], cw, layer, height)
             return carry
 
-        lax.fori_loop(0, cols // CH, step, 0)
-
-    interior(xin, y1, 0, 1, 2)
+        lax.fori_loop(0, count, step, 0)
+
+    full = cols // CH
+    interior(xin, y1, 0, 1, 2, full)
     pl.semaphore_wait(barrier, 6)
 
     messages = []
@@ -186,17 +189,20 @@
         send(window.at[pl.ds(start, edge)], window.at[pl.ds(start + 2 * sec, edge)], -2)
 
     fetches[1].wait()
-    interior(y1, y2, 1, 2, 1)
+    interior(y1, y2, 1, 2, 1, full - 1)
     fetches[2].wait()
-    interior(y2, feats, 2, 3, 0)
+    interior(y2, feats, 2, 3, 0, full - 2)
 
     messages[0].wait_recv()
     messages[1].wait_recv()
-    for layer, (src, dst, extra) in enumerate(((xin, y1, 4), (y1, y2, 2), (y2, feats, 0))):
-        right = (cols + extra - 3) * height
-        edge = conv_rows(src, [0, right], h3, cw, layer, height)
+    for layer, (src, dst, extra, done) in enumerate(
+        ((xin, y1, 4, cols - 2), (y1, y2, 2, cols - CH), (y2, feats, 0, cols - 2 * CH))
+    ):
+        right = (3 + done) * height
+        size = (cols + extra) * height - right
+        edge = conv_rows(src, [(0, h3), (right, size)], cw, layer, height)
         dst[pl.ds(0, h3), :] = edge[:h3]
-        dst[pl.ds(right, h3), :] = edge[h3:]
+        dst[pl.ds(right, size), :] = edge[h3:]
 
     outs = []
 
@@ -423,9 +429,10 @@
             jax.ShapeDtypeStruct((rows, lanes), f32),
             jax.ShapeDtypeStruct((rows, lanes), f32),
         ),
-        in_specs=[vm, hbm, vm, vm, vm, vm, vm, vm, hbm],
+        in_specs=[hbm, hbm, vm, vm, vm, vm, vm, vm, hbm],
         out_specs=(vm,) * 4 + (hbm,) * 4,
         scratch_shapes=[
+            pltpu.VMEM(image_feats.shape, bf),
             pltpu.VMEM(cam_weights.shape, bf),
             pltpu.VMEM(merge_weight.shape, bf),
             pltpu.VMEM(((cols + 6) * height, channels), bf),
@@ -450,7 +457,7 @@
             pltpu.VMEM((total, channels), f32),
             pltpu.VMEM((total, cl), bf),
             pltpu.VMEM((total - 2 * br, cf), bf),
-            pltpu.SemaphoreType.DMA((cam_weights.shape[0] + 1,)),
+            pltpu.SemaphoreType.DMA((cam_weights.shape[0] + 2,)),
             pltpu.SemaphoreType.DMA((4,)),
             pltpu.SemaphoreType.DMA((16,)),
             pltpu.SemaphoreType.DMA((16,)),

time: 42.6 us -> 41.8 us (0.981)
  Pallas kernels: 41.8 us -> 41 us
    pallas_call x1, Pallas kernels: 34.1 us -> 33.3 us  [local(): pl.pallas_call(functools.partial(kernel, n, strips, cols, height, br, ba,...]
where the time goes in v5:
time: 41.8 us; the launch traced here: 41.6 us
  Pallas kernels  41 us (98%)
  between operations  0.64 us (2%)
    pallas_call x1, Pallas kernels, local(): pl.pallas_call(functools.partial(kernel, n, strips, cols, height, br, ba,...  33.3 us
    pallas_call x1, Pallas kernels, local(): pl.pallas_call(functools.partial(back_kernel, height, bins_n), grid=(step...  7.64 us

profile of v5, /device:TPU:0, one launch (start us, length us, event | category | flops | bytes accessed | tf_op | source)
XLA Modules:
  0.0 41.6 jit_solution(6210703734192857377)
XLA Ops:
  0.6 33.3 %bev.1 = (bf16[16,4,256]{2,1,0:T(4,128)(2,1)}, bf16[16,4,128]{2,1,0:T(4,128)(2,1)}, bf16[192,256]{1,0:T(8,128)(2,1)}, f32[64,128]{1,0:T(8,128)}, bf16[2048,256]{...) custom-call(bf16[32,64,256]{2,1,0:T(8,128)(2,1)} %img_hbm.1, ...), custom_call_target="tpu_custom_call" | custom-call | tf_op jit(solution)/shard_map/bev/pallas_call | solution.py:420
  34.0 7.6 %back.1 = (bf16[32,64,256]{2,1,0:T(8,128)(2,1)}, bf16[16,4,256]{2,1,0:T(4,128)(2,1)}, bf16[16,4,128]{2,1,0:T(4,128)(2,1)}) custom-call(bf16[2048,256]{1,0:T(8,128)(2,1)} %get-tuple-element.14.feats, bf16[2048,192]{1,0:T(8,128)(2,1)} %get-tuple-element.15.amat, f32[2048,128]{1,0:T(8,128)} %get-tuple-element.16.probs, f32[2048,128]{1,0:T(8,128)} %get-tuple-element.17.slope, ...), custom_call_target="tpu_custom_call" | custom-call | tf_op jit(solution)/shard_map/back/pallas_call | solution.py:481
